TPU v7x, 512 devices: a whole 4x8x8 slice. The times are simulated.
512 devices in a mesh: cell: 64 (over z, x, y_lo), aux: 8 (over y_hi, core).
Axes of the slice: x: 4, y: 8 (y_hi: 4, y_lo: 2; y = y_hi * 2 + y_lo), z: 8, core: 2. Of those that a mesh axis runs over, the one named last changes fastest.
Arguments:
- blocks: float32 [64, 32, 300, 300], P('cell', 'aux'), may hold values from -0.75 to 0.75
- cell_offsets: int32 [3, 64], replicated, may hold values from -2 to 1, as said below
- occ_coeff: float32 [2, 300, 60], replicated, may hold values from -0.25 to 0.25
- vir_coeff: float32 [64, 2, 300, 240], P('cell', None, None, 'aux'), may hold values from -0.25 to 0.25
- transfer_index: int32 [64], replicated, may hold values from 0 to 63, as said below
Outputs:
- pair_ints: float32 [2, 32, 64, 14400], P(None, 'aux', None, 'cell')
Inputs may be any that keep to these rules, and one draw needn't show every extreme that they name: `cell_offsets`: column R is the integer lattice vector of cell R; the columns are the 64 cells of the centred 4 x 4 x 4 supercell, each once, in an order drawn from the seed. `transfer_index`: entry k is the index (a 4 + b) * 4 + c of the k-point k - k1 folded into the 4 x 4 x 4 mesh, for one k1 drawn from the seed; every index appears once.
All inputs are finite; a program needn't handle non-finite values.
Results may differ from a plain program's by a relative error of at most 0.00007.
Values sent between devices are 32-bit elements; how exact they have to be, the bound alone decides.
A program may use at most 64 MiB of HBM per device.

v0:
```python
import math

import jax
import jax.numpy as jnp
from jax import lax
from jax.sharding import PartitionSpec as P

KX = 4
KY = 4


def cut_along(shard, dim, length):
    before, after = (shard.shape[:dim], shard.shape[dim + 1 :])
    return jnp.moveaxis(shard.reshape(*before, length, -1, *after), dim, 0)


def piece_ends(length, count):
    unit = 8 if length >= 8 * count else 1
    return [length // unit * k // count * unit for k in range(1, count)]


def laid_out(tiles, dim):
    dims = list(tiles.shape[1:])
    dims[dim] *= tiles.shape[0]
    return jnp.moveaxis(tiles, 0, dim).reshape(dims)


def cut_exchange(shard, axis, pieces, split_dim, concat_dim):
    tiles = cut_along(shard, split_dim, lax.axis_size(axis))
    split_at = max(range(1, max(2, tiles.ndim - 1)), key=lambda d: tiles.shape[d])
    done = []
    for section in jnp.split(tiles, piece_ends(tiles.shape[split_at], pieces), axis=split_at):
        if section.size:
            done.append(lax.all_to_all(section, axis, split_axis=0, concat_axis=0, tiled=True))
    return laid_out(jnp.concatenate(done, axis=split_at), concat_dim)


def copy_for_each(shard, axis):
    length = lax.axis_size(axis)
    return lax.all_to_all(
        jnp.broadcast_to(shard[None], (length, *shard.shape)), axis, 0, 0, tiled=True
    )


def gathered_copies(shard, axis, dim):
    tiles = copy_for_each(shard, axis)
    return laid_out(tiles, dim)


def phase_tables(cell_offsets, cell_count):
    depth = cell_count // (KX * KY)
    points = jnp.arange(cell_count, dtype=jnp.int32)
    along_a = points // (KY * depth)
    along_b = points // depth % KY
    along_c = points % depth
    turns = (
        along_a[:, None] * cell_offsets[0][None, :] * (KY * depth)
        + along_b[:, None] * cell_offsets[1][None, :] * (KX * depth)
        + along_c[:, None] * cell_offsets[2][None, :] * (KX * KY)
    ) % cell_count
    angles = 2.0 * math.pi / cell_count * turns.astype(jnp.float32)
    return (jnp.cos(angles), jnp.sin(angles))


def matmul(left, right):
    return jnp.dot(left, right, precision=lax.Precision.HIGHEST, preferred_element_type=jnp.float32)


def contract(form, left, right):
    return jnp.einsum(form, left, right, precision=lax.Precision.HIGHEST)


def on_device(blocks, cell_offsets, occ_coeff, vir_coeff, transfer_index):
    cell_count = lax.axis_size("cell")
    slab_rows = blocks.shape[1]
    basis_size = blocks.shape[2]
    occupied = occ_coeff.shape[2]
    cosines, sines = phase_tables(cell_offsets, cell_count)
    occ_real, occ_imag = (occ_coeff[0], occ_coeff[1])
    own_blocks = blocks[0]
    half_real = contract("mi,pmn->pin", occ_real, own_blocks)
    half_imag = -contract("mi,pmn->pin", occ_imag, own_blocks)
    packed = jnp.stack([half_real, half_imag]).reshape(2, 1, -1)
    arrived = cut_exchange(packed, "cell", 2, 2, 1)
    spec_real = matmul(cosines, arrived[0]) - matmul(sines, arrived[1])
    spec_imag = matmul(sines, arrived[0]) + matmul(cosines, arrived[1])
    returned = lax.all_to_all(
        jnp.stack([spec_real, spec_imag]), "cell", split_axis=1, concat_axis=2, tiled=True
    )
    spectra = returned.reshape(2, slab_rows, occupied, basis_size)
    half_real, half_imag = (spectra[0], spectra[1])
    rows_real = half_real.reshape(slab_rows * occupied, basis_size)
    rows_imag = half_imag.reshape(slab_rows * occupied, basis_size)
    column_piece = gathered_copies(vir_coeff, "aux", 3)
    coef_real = column_piece[0, 0]
    coef_imag = column_piece[0, 1]
    part_real = matmul(rows_real, coef_real) - matmul(rows_imag, coef_imag)
    part_imag = matmul(rows_real, coef_imag) + matmul(rows_imag, coef_real)
    banded = jnp.stack([part_real, part_imag])
    pair_rows = banded.reshape(2, slab_rows, 1, -1)
    regrouped = lax.all_to_all(pair_rows, "cell", split_axis=3, concat_axis=2, tiled=True)
    source = jnp.argsort(transfer_index)
    return jnp.take(regrouped, source, axis=2)


def solution(mesh):
    placed = (P("cell", "aux", None, None), P(), P(), P("cell", None, None, "aux"), P())
    return jax.shard_map(
        on_device,
        mesh=mesh,
        in_specs=placed,
        out_specs=P(None, "aux", None, "cell"),
        check_vma=False,
    )
```

profile of v0, /device:TPU:1, one launch (start us, length us, event | category | flops | bytes accessed | tf_op | source)
XLA Modules:
  0.0 196.1 jit_solution(14375192744590007590)
XLA Ops:
  0.0 1.3 fusion.64
  1.3 3.1 %fusion.6 = f32[4,60,300]{2,1,0:T(8,128)S(1)} fusion(f32[4,300,300]{2,0,1:T(4,128)} %bitcast.62, f32[1,300,60]{1,0,2:T(1,128)S(1)} %get-tuple-element.15), kind=kOutput, calls=%fused_computation.9 | convolution fusion | flops 259200000 | bytes 1800000 | tf_op jit(solution)/shard_map/mi,pmn->pin/dot_general | solution.py:70
  4.7 1.6 fusion.12
  6.7 1.0 copy.44
  7.7 15.3 %all-to-all-start = ((f32[64,1,1,1125]{3,2,1,0:T(1,128)}), f32[64,1,1,1125]{3,2,1,0:T(1,128)S(1)}, u32[]{:S(2)}, u32[]{:S(2)}) async-start(f32[64,1,1,1125]{3,2,1,0:T(1,128)} %copy.44), calls=%async_computation | async-start | bytes 589824 | tf_op jit(solution)/shard_map/all_to_all | solution.py:34
  23.0 1.0 copy.45
  24.0 10.5 %all-to-all-done = f32[64,1,1,1125]{3,2,1,0:T(1,128)S(1)} async-done(((f32[64,1,1,1125]{3,2,1,0:T(1,128)}), f32[64,1,1,1125]{3,2,1,0:T(1,128)S(1)}, u32[]{:S(2)}, u32[]{:S(2)}) %all-to-all-start) | async-done | bytes 288032 | tf_op jit(solution)/shard_map/all_to_all | solution.py:34
  34.5 6.9 %all-to-all-start.1 = ((f32[64,1,1,1125]{3,2,1,0:T(1,128)}), f32[64,1,1,1125]{3,2,1,0:T(1,128)S(1)}, u32[]{:S(2)}, u32[]{:S(2)}) async-start(f32[64,1,1,1125]{3,2,1,0:T(1,128)} %copy.45), calls=%async_computation.1 | async-start | bytes 589824 | tf_op jit(solution)/shard_map/all_to_all | solution.py:34
  41.5 11.5 %all-to-all-done.1 = f32[64,1,1,1125]{3,2,1,0:T(1,128)S(1)} async-done(((f32[64,1,1,1125]{3,2,1,0:T(1,128)}), f32[64,1,1,1125]{3,2,1,0:T(1,128)S(1)}, u32[]{:S(2)}, u32[]{:S(2)}) %all-to-all-start.1) | async-done | bytes 288032 | tf_op jit(solution)/shard_map/all_to_all | solution.py:34
  53.0 1.1 broadcast_in_dim.25
  54.1 9.3 %all-to-all-start.3 = ((f32[8,1,2,300,30]{3,2,4,1,0:T(2,128)}), f32[8,1,2,300,30]{3,2,4,1,0:T(2,128)S(1)}, u32[]{:S(2)}, u32[]{:S(2)}) async-start(f32[8,1,2,300,30]{3,2,4,1,0:T(2,128)} %broadcast_in_dim.25), calls=%async_computation.3 | async-start | bytes 1474560 | tf_op jit(solution)/shard_map/all_to_all | solution.py:40
  64.0 0.6 fusion.25
  64.6 0.6 fusion
  65.2 0.6 fusion.23
  65.8 0.6 fusion.1
  66.4 1.3 copy.46
  67.7 13.9 %all-to-all-done.3 = f32[8,1,2,300,30]{3,2,4,1,0:T(2,128)S(1)} async-done(((f32[8,1,2,300,30]{3,2,4,1,0:T(2,128)}), f32[8,1,2,300,30]{3,2,4,1,0:T(2,128)S(1)}, u32[]{:S(2)}, u32[]{:S(2)}) %all-to-all-start.3) | async-done | bytes 576032 | tf_op jit(solution)/shard_map/all_to_all | solution.py:40
  81.6 8.0 %all-to-all-start.2 = ((f32[2,64,1125]{2,0,1:T(2,128)}), f32[2,64,1125]{2,0,1:T(2,128)S(1)}, u32[]{:S(2)}, u32[]{:S(2)}) async-start(f32[2,64,1125]{2,0,1:T(2,128)} %copy.46), calls=%async_computation.2 | async-start | bytes 1179648 | tf_op jit(solution)/shard_map/all_to_all | solution.py:87
  90.2 0.6 copy.47
  90.8 0.6 copy.48
  91.4 15.3 %all-to-all-done.2 = f32[2,64,1125]{2,0,1:T(2,128)S(1)} async-done(((f32[2,64,1125]{2,0,1:T(2,128)}), f32[2,64,1125]{2,0,1:T(2,128)S(1)}, u32[]{:S(2)}, u32[]{:S(2)}) %all-to-all-start.2) | async-done | bytes 576032 | tf_op jit(solution)/shard_map/all_to_all | solution.py:87
  106.7 1.6 slice_reduce_fusion
  111.7 13.5 %copy.49 = f32[2,4,1,14400]{1,0,2,3:T(2,128)} copy(f32[2,4,1,14400]{3,1,2,0:T(4,128)S(1)} %pad_maximum_fusion.1) | data formatting | bytes 921600 | tf_op jit(solution)/shard_map/stack | solution.py:99
  125.2 16.7 %reshape.97 = f32[64,1,1800]{2,1,0:T(1,128)} reshape(f32[14400,1,2,4]{3,2,1,0:T(2,128)} %bitcast.60) | data formatting | bytes 921600
  141.9 7.5 %all-to-all-start.4 = ((f32[64,1,1800]{2,1,0:T(1,128)}), f32[64,1,1800]{2,1,0:T(1,128)S(1)}, u32[]{:S(2)}, u32[]{:S(2)}) async-start(f32[64,1,1800]{2,1,0:T(1,128)} %reshape.97), calls=%async_computation.4 | async-start | bytes 983040 | tf_op jit(solution)/shard_map/all_to_all | solution.py:101
  149.5 2.0 %sort.17 = (s32[64]{0:T(128)}, s32[64]{0:T(128)S(1)}) sort(s32[64]{0:T(128)S(1)} %copy-done.3, s32[64]{0:T(128)S(1)} %iota.20), dimensions={0}, to_apply=%region_0.1 | sort | flops 384 | bytes 1024 | tf_op jit(solution)/shard_map/jit(argsort)/sort | solution.py:102
  151.6 13.3 %all-to-all-done.4 = f32[64,1,1800]{2,1,0:T(1,128)S(1)} async-done(((f32[64,1,1800]{2,1,0:T(1,128)}), f32[64,1,1800]{2,1,0:T(1,128)S(1)}, u32[]{:S(2)}, u32[]{:S(2)}) %all-to-all-start.4) | async-done | bytes 460832 | tf_op jit(solution)/shard_map/all_to_all | solution.py:101
  165.4 1.8 reduce.4
  167.2 11.2 %reshape.98 = f32[14400,1,2,4]{3,2,1,0:T(2,128)} reshape(f32[64,1800]{1,0:T(8,128)S(1)} %reduce.4) | data formatting | bytes 921600
  178.4 15.7 %copy.51 = f32[2,4,64,225]{3,1,2,0:T(4,128)S(1)} copy(f32[2,4,64,225]{1,0,3,2:T(2,128)} %bitcast.61) | data formatting | bytes 921600 | tf_op jit(solution)/shard_map/all_to_all | solution.py:101
  194.1 0.9 gather_fusion
  195.1 1.0 copy.52
  (34 shorter events, 6.0 us)
Async XLA Ops:
  0.0 4.7 %copy-start = (f32[1,4,300,300]{3,1,2,0:T(4,128)S(1)}, f32[1,4,300,300]{3,1,2,0:T(4,128)}, u32[]{:S(2)}) copy-start(f32[1,4,300,300]{3,1,2,0:T(4,128)} %param.5) | copy-start | bytes 4320004
  6.6 34.9 %copy-start.2 = (s32[3,64]{1,0:T(4,128)S(1)}, s32[3,64]{1,0:T(4,128)}, u32[]{:S(2)}) copy-start(s32[3,64]{1,0:T(4,128)} %param.6) | copy-start | bytes 2308
  6.6 46.4 %copy-start.1 = (f32[1,2,300,30]{2,1,3,0:T(2,128)S(1)}, f32[1,2,300,30]{2,1,3,0:T(2,128)}, u32[]{:S(2)}) copy-start(f32[1,2,300,30]{2,1,3,0:T(2,128)} %param.8) | copy-start | bytes 216004
  7.7 26.8 %all-to-all-start = ((f32[64,1,1,1125]{3,2,1,0:T(1,128)}), f32[64,1,1,1125]{3,2,1,0:T(1,128)S(1)}, u32[]{:S(2)}, u32[]{:S(2)}) async-start(f32[64,1,1,1125]{3,2,1,0:T(1,128)} %copy.44), calls=%async_computation | async-start | bytes 589824 | tf_op jit(solution)/shard_map/all_to_all | solution.py:34
  34.5 18.5 %all-to-all-start.1 = ((f32[64,1,1,1125]{3,2,1,0:T(1,128)}), f32[64,1,1,1125]{3,2,1,0:T(1,128)S(1)}, u32[]{:S(2)}, u32[]{:S(2)}) async-start(f32[64,1,1,1125]{3,2,1,0:T(1,128)} %copy.45), calls=%async_computation.1 | async-start | bytes 589824 | tf_op jit(solution)/shard_map/all_to_all | solution.py:34
  54.1 27.5 %all-to-all-start.3 = ((f32[8,1,2,300,30]{3,2,4,1,0:T(2,128)}), f32[8,1,2,300,30]{3,2,4,1,0:T(2,128)S(1)}, u32[]{:S(2)}, u32[]{:S(2)}) async-start(f32[8,1,2,300,30]{3,2,4,1,0:T(2,128)} %broadcast_in_dim.25), calls=%async_computation.3 | async-start | bytes 1474560 | tf_op jit(solution)/shard_map/all_to_all | solution.py:40
  81.6 25.1 %all-to-all-start.2 = ((f32[2,64,1125]{2,0,1:T(2,128)}), f32[2,64,1125]{2,0,1:T(2,128)S(1)}, u32[]{:S(2)}, u32[]{:S(2)}) async-start(f32[2,64,1125]{2,0,1:T(2,128)} %copy.46), calls=%async_computation.2 | async-start | bytes 1179648 | tf_op jit(solution)/shard_map/all_to_all | solution.py:87
  125.2 24.3 %copy-start.3 = (s32[64]{0:T(128)S(1)}, s32[64]{0:T(128)}, u32[]{:S(2)}) copy-start(s32[64]{0:T(128)} %param.9) | copy-start | bytes 772
  141.9 23.0 %all-to-all-start.4 = ((f32[64,1,1800]{2,1,0:T(1,128)}), f32[64,1,1800]{2,1,0:T(1,128)S(1)}, u32[]{:S(2)}, u32[]{:S(2)}) async-start(f32[64,1,1800]{2,1,0:T(1,128)} %reshape.97), calls=%async_computation.4 | async-start | bytes 983040 | tf_op jit(solution)/shard_map/all_to_all | solution.py:101
where the time goes:
time: 197 us; the launch traced here: 196 us
  local copies, waits for them, and re-layouts  70.2 us (36%)
  waiting for transfers between devices  64.5 us (33%)
  starting transfers between devices  47.1 us (24%)
  matrix products  9.13 us (5%)
  other arithmetic  4.77 us (2%)
    unnamed x10, local copies, waits for them, and re-layouts  27.9 us
    all_to_all x2, starting transfers between devices, cut_exchange(): lax.all_to_all(section, axis, split_axis=0, concat_axis=0, tiled=True)  22.3 us
    all_to_all x2, waiting for transfers between devices, cut_exchange(): lax.all_to_all(section, axis, split_axis=0, concat_axis=0, tiled=True)  22 us
    all_to_all x2, local copies, waits for them, and re-layouts, on_device(): lax.all_to_all(pair_rows, 'cell', split_axis=3, concat_axis=2, tiled=True)  16.2 us
    all_to_all x1, waiting for transfers between devices, on_device(): lax.all_to_all(jnp.stack([spec_real, spec_imag]), 'cell', split_axis=1, c...  15.3 us
    another operation x3, local copies, waits for them, and re-layouts, on_device(): banded = jnp.stack([part_real, part_imag])  13.9 us
    all_to_all x1, waiting for transfers between devices, copy_for_each(): lax.all_to_all(jnp.broadcast_to(shard[None], (length, *shard.shape)), axi...  13.9 us
    all_to_all x1, waiting for transfers between devices, on_device(): lax.all_to_all(pair_rows, 'cell', split_axis=3, concat_axis=2, tiled=True)  13.3 us
  transfers between devices with their start and end apart: 5, of which 5 were waited for; matrix products, arithmetic and copies ran while one was open for 5% of the time, Pallas kernels for 0%

commit v1 on v0

v1 whole, which is shorter than its diff:
```python
import functools

import jax
import jax.numpy as jnp
from jax import lax
from jax.experimental import pallas as pl
from jax.experimental.pallas import tpu as pltpu
from jax.sharding import PartitionSpec as P

CELLS = 64
AUX = 8
NB = 300
NO = 60
NV = 240
ROWS = 4
LANES = 128
TILES = 3
GROUP = 16
WORKERS = 60
PAIRS = 225
MESH = pl.DeviceIdType.MESH
F32 = jnp.float32
BF16 = jnp.bfloat16


def split(x):
    high = x.astype(BF16)
    low = (x - high.astype(F32)).astype(BF16)
    return high, low


def dot(a, b, transposed=False):
    dims = (((1,), (1 if transposed else 0,)), ((), ()))
    return lax.dot_general(a, b, dims, preferred_element_type=F32)


def dot3(a, b, transposed=False):
    return (
        dot(a[0], b[0], transposed)
        + dot(a[0], b[1], transposed)
        + dot(a[1], b[0], transposed)
    )


def tile_lanes(tile):
    return LANES if tile < TILES - 1 else NB - LANES * (TILES - 1)


def quarter_turns():
    row = lax.broadcasted_iota(jnp.int32, (8, LANES), 0)
    return jnp.where(row < ROWS, -1.0, 1.0).astype(F32)


def times_i(x, sign):
    return pltpu.roll(x, ROWS, 0) * sign


def four_points(x, sign):
    even, odd = x[0] + x[2], x[1] + x[3]
    left, right = x[0] - x[2], times_i(x[1] - x[3], sign)
    return even + odd, left + right, even - odd, left - right


def kernel(
    pos, blocks, occ, vir, out,
    occ_v, blocks_v, sent_half, got_half_0, got_half_1, got_half_2, middle, sent_spec, got_spec,
    vir_own, vir_all, vir_rows, vir_high, vir_low, band, sent_pairs,
    load_sem, vir_load_sem, half_send, half_recv, half_local, spec_send, spec_recv, spec_local,
    pair_send, pair_recv, pair_local, vir_send, vir_recv, vir_local,
):
    got_half = (got_half_0, got_half_1, got_half_2)
    me = lax.axis_index("cell")
    my_aux = lax.axis_index("aux")
    active = lax.rem(me, GROUP) != GROUP - 1
    my_slot = me - me // GROUP

    barrier = pltpu.get_barrier_semaphore()

    def greet(j, carry):
        pl.semaphore_signal(
            barrier, inc=1, device_id={"cell": lax.rem(me + j, CELLS)}, device_id_type=MESH
        )
        return carry

    lax.fori_loop(1, CELLS, greet, 0)

    def greet_aux(j, carry):
        pl.semaphore_signal(
            barrier, inc=1, device_id={"aux": lax.rem(my_aux + j, AUX)}, device_id_type=MESH
        )
        return carry

    lax.fori_loop(1, AUX, greet_aux, 0)

    occ_loads = [pltpu.make_async_copy(occ.at[:, t, :], occ_v.at[t], load_sem.at[t]) for t in range(2)]
    block_loads = [pltpu.make_async_copy(blocks.at[:, p, :], blocks_v.at[p], load_sem.at[2 + p]) for p in range(ROWS)]
    for load in occ_loads + block_loads:
        load.start()
    vir_load = pltpu.make_async_copy(vir, vir_own, vir_load_sem)
    vir_load.start()

    for load in occ_loads:
        load.wait()
    blank = jnp.zeros((64 - NO, NB), F32)
    left_rows = jnp.concatenate([occ_v[0], blank, -occ_v[1], blank], axis=0)
    left = split(left_rows)
    for load in block_loads:
        load.wait()

    def half_product(tile):
        width = tile_lanes(tile)
        for pair in range(ROWS // 2):
            parts = []
            for p in (2 * pair, 2 * pair + 1):
                part = blocks_v[p, :, tile * LANES : tile * LANES + width]
                if width < LANES:
                    part = jnp.concatenate([part, jnp.zeros((NB, LANES - width), F32)], axis=1)
                parts.append(part)
            product = dot3(left, split(jnp.concatenate(parts, axis=1)))
            for at in range(2):
                for t in range(2):
                    rows = product[t * 64 : t * 64 + NO, at * LANES : (at + 1) * LANES]
                    sent_half[tile, pl.ds(t * ROWS + 2 * pair + at, NO, stride=8), :] = rows

    def send_half(tile):
        def one(j, carry):
            peer = lax.rem(me + j, CELLS)
            slot = peer - peer // GROUP

            @pl.when(lax.rem(peer, GROUP) != GROUP - 1)
            def _():
                pltpu.make_async_remote_copy(
                    src_ref=sent_half.at[tile, pl.ds(pl.multiple_of(slot * 8, 8), 8)],
                    dst_ref=got_half[tile].at[me],
                    send_sem=half_send.at[tile],
                    recv_sem=half_recv.at[tile],
                    device_id={"cell": peer},
                    device_id_type=MESH,
                ).start()

            return carry

        lax.fori_loop(1, CELLS, one, 0)

        @pl.when(active)
        def _():
            pltpu.make_async_copy(
                sent_half.at[tile, pl.ds(pl.multiple_of(my_slot * 8, 8), 8)], got_half[tile].at[me], half_local.at[tile]
            ).start()

    half_product(0)
    pl.semaphore_wait(barrier, CELLS - 1 + AUX - 1)
    send_half(0)
    for tile in range(1, TILES):
        half_product(tile)
        send_half(tile)

    vir_load.wait()

    def send_vir(j, carry):
        pltpu.make_async_remote_copy(
            src_ref=vir_own,
            dst_ref=vir_all.at[pl.ds(my_aux * (NV // AUX), NV // AUX)],
            send_sem=vir_send,
            recv_sem=vir_recv,
            device_id={"aux": lax.rem(my_aux + j, AUX)},
            device_id_type=MESH,
        ).start()
        return carry

    lax.fori_loop(1, AUX, send_vir, 0)
    own_vir = pltpu.make_async_copy(vir_own, vir_all.at[pl.ds(my_aux * (NV // AUX), NV // AUX)], vir_local)
    own_vir.start()

    sign = quarter_turns()

    def wait_bytes(ref, sem):
        pltpu.make_async_copy(ref, ref, sem).wait()

    def fourier(tile):
        wait_bytes(got_half[tile].at[pl.ds(0, CELLS - 1)], half_recv.at[tile])
        wait_bytes(got_half[tile].at[0], half_local.at[tile])
        for c in range(4):
            x = [[got_half[tile][pos[a * 16 + b * 4 + c]] for b in range(4)] for a in range(4)]
            columns = [four_points([x[a][b] for a in range(4)], sign) for b in range(4)]
            for a in range(4):
                y = four_points([columns[b][a] for b in range(4)], sign)
                for b in range(4):
                    middle[a * 16 + b * 4 + c] = y[b]
        for at in range(16):
            y = four_points([middle[at * 4 + c] for c in range(4)], sign)
            for c in range(4):
                sent_spec[tile, at * 4 + c] = y[c]

        def one(j, carry):
            peer = lax.rem(me + j, CELLS)
            pltpu.make_async_remote_copy(
                src_ref=sent_spec.at[tile, peer],
                dst_ref=got_spec.at[tile, my_slot],
                send_sem=spec_send.at[tile],
                recv_sem=spec_recv.at[tile],
                device_id={"cell": peer},
                device_id_type=MESH,
            ).start()
            return carry

        lax.fori_loop(1, CELLS, one, 0)
        pltpu.make_async_copy(sent_spec.at[tile, me], got_spec.at[tile, my_slot], spec_local.at[tile]).start()

    @pl.when(active)
    def _():
        for tile in range(TILES):
            fourier(tile)

    own_vir.wait()
    wait_bytes(vir_all.at[pl.ds(0, NV - NV // AUX)], vir_recv)
    spread = [pltpu.make_async_copy(vir_all.at[:, t, :], vir_rows.at[t], load_sem.at[t]) for t in range(2)]
    for copy in spread:
        copy.start()
    for copy in spread:
        copy.wait()
    for tile in range(TILES):
        width = tile_lanes(tile)
        for t in range(2):
            part = vir_rows[t, :, tile * LANES : tile * LANES + width]
            if width < LANES:
                part = jnp.concatenate([part, jnp.zeros((NV, LANES - width), F32)], axis=1)
            high, low = split(part)
            vir_high[tile, :, t * LANES : (t + 1) * LANES] = high
            vir_low[tile, :, t * LANES : (t + 1) * LANES] = low

    per_group = WORKERS // 4

    def wait_spec(tile):
        @pl.when(active)
        def _():
            wait_bytes(got_spec.at[tile, pl.ds(0, WORKERS - 1)], spec_recv.at[tile])
            wait_bytes(got_spec.at[tile, 0], spec_local.at[tile])

        @pl.when(jnp.logical_not(active))
        def _():
            wait_bytes(got_spec.at[tile, pl.ds(0, WORKERS)], spec_recv.at[tile])

    def partial_band(tile, group):
        x = got_spec[tile, pl.ds(group * per_group, per_group)]
        turned = jnp.stack([times_i(x[n], sign) for n in range(per_group)])
        both = jnp.concatenate([x.reshape(per_group * 8, LANES), turned.reshape(per_group * 8, LANES)], axis=1)
        return dot3(split(both), (vir_high[tile], vir_low[tile]), transposed=True)

    rows_per_group = per_group * 8
    for tile in range(TILES - 1):
        wait_spec(tile)

        def accumulate(group, carry):
            at = pl.ds(pl.multiple_of(group * rows_per_group, 8), rows_per_group)
            value = partial_band(tile, group)
            if tile:
                value = band[at, :] + value
            band[at, :] = value
            return carry

        lax.fori_loop(0, 4, accumulate, 0)

    wait_spec(TILES - 1)
    lane = lax.broadcasted_iota(jnp.int32, (8, 2 * LANES), 1)

    def finish(group, carry):
        at = pl.ds(pl.multiple_of(group * rows_per_group, 8), rows_per_group)
        value = band[at, :] + partial_band(TILES - 1, group)
        wide = jnp.concatenate([value, jnp.zeros((rows_per_group, 2 * LANES - NV), F32)], axis=1)
        wide = wide.reshape(per_group, 8, 2 * LANES)
        for m in range(GROUP):
            shift = (NV - PAIRS) * m
            if m == 0:
                chunk = wide[0]
            else:
                chunk = pltpu.roll(wide[m - 1], 2 * LANES - (NV - shift), 1)
                if m < GROUP - 1:
                    chunk = jnp.where(lane < shift, chunk, pltpu.roll(wide[m], shift, 1))
            sent_pairs[group * GROUP + m] = chunk

        def one(m, inner):
            peer = group * GROUP + m

            @pl.when(peer != me)
            def _():
                pltpu.make_async_remote_copy(
                    src_ref=sent_pairs.at[peer],
                    dst_ref=out.at[me],
                    send_sem=pair_send,
                    recv_sem=pair_recv,
                    device_id={"cell": peer},
                    device_id_type=MESH,
                ).start()

            @pl.when(peer == me)
            def _():
                pltpu.make_async_copy(sent_pairs.at[peer], out.at[peer], pair_local).start()

            return inner

        lax.fori_loop(0, GROUP, one, 0)
        return carry

    lax.fori_loop(0, 4, finish, 0)

    for tile in range(TILES):
        @pl.when(active)
        def _():
            wait_bytes(sent_half.at[tile, pl.ds(0, (WORKERS - 1) * 8)], half_send.at[tile])
            wait_bytes(sent_spec.at[tile, pl.ds(0, CELLS - 1)], spec_send.at[tile])

        @pl.when(jnp.logical_not(active))
        def _():
            wait_bytes(sent_half.at[tile], half_send.at[tile])

    wait_bytes(vir_all.at[pl.ds(0, NV - NV // AUX)], vir_send)
    wait_bytes(sent_pairs.at[pl.ds(0, CELLS - 1)], pair_send)
    wait_bytes(out.at[0], pair_local)
    wait_bytes(out.at[pl.ds(0, CELLS - 1)], pair_recv)


def exchange(pos, blocks, occ, vir):
    dma = pltpu.SemaphoreType.DMA
    return pl.pallas_call(
        kernel,
        out_shape=jax.ShapeDtypeStruct((CELLS, 8, 2 * LANES), F32),
        in_specs=[
            pl.BlockSpec(memory_space=pltpu.SMEM),
            pl.BlockSpec(memory_space=pl.ANY),
            pl.BlockSpec(memory_space=pl.ANY),
            pl.BlockSpec(memory_space=pl.ANY),
        ],
        out_specs=pl.BlockSpec(memory_space=pltpu.VMEM),
        scratch_shapes=[
            pltpu.VMEM((2, NO, NB), F32),
            pltpu.VMEM((ROWS, NB, NB), F32),
            pltpu.VMEM((TILES, WORKERS * 8, LANES), F32),
            pltpu.VMEM((CELLS, 8, LANES), F32),
            pltpu.VMEM((CELLS, 8, LANES), F32),
            pltpu.VMEM((CELLS, 8, LANES), F32),
            pltpu.VMEM((CELLS, 8, LANES), F32),
            pltpu.VMEM((TILES, CELLS, 8, LANES), F32),
            pltpu.VMEM((TILES, WORKERS, 8, LANES), F32),
            pltpu.VMEM((NV // AUX, 2, NB), F32),
            pltpu.VMEM((NV, 2, NB), F32),
            pltpu.VMEM((2, NV, NB), F32),
            pltpu.VMEM((TILES, NV, 2 * LANES), BF16),
            pltpu.VMEM((TILES, NV, 2 * LANES), BF16),
            pltpu.VMEM((WORKERS * 8, NV), F32),
            pltpu.VMEM((CELLS, 8, 2 * LANES), F32),
            dma((2 + ROWS,)),
            dma,
            dma((TILES,)),
            dma((TILES,)),
            dma((TILES,)),
            dma((TILES,)),
            dma((TILES,)),
            dma((TILES,)),
            dma,
            dma,
            dma,
            dma,
            dma,
            dma,
        ],
        compiler_params=pltpu.CompilerParams(
            collective_id=0, has_side_effects=True, vmem_limit_bytes=63 << 20
        ),
        name="transform",
    )(pos, blocks, occ, vir)


def inverse(order):
    index = jnp.arange(CELLS, dtype=jnp.int32)
    return jnp.sum(jnp.where(order[None, :] == index[:, None], index[None, :], 0), axis=1)


def on_device(blocks, cell_offsets, occ_coeff, vir_coeff, transfer_index):
    folded = cell_offsets & 3
    pos = inverse(folded[0] * 16 + folded[1] * 4 + folded[2])
    got = exchange(
        pos,
        jnp.transpose(blocks[0], (1, 0, 2)),
        jnp.transpose(occ_coeff, (2, 0, 1)),
        jnp.transpose(vir_coeff[0], (2, 0, 1)),
    )
    source = inverse(transfer_index)
    ordered = jnp.take(got, source, axis=0)[:, :, :PAIRS]
    return jnp.transpose(ordered.reshape(CELLS, 2, ROWS, PAIRS), (1, 2, 0, 3))


def solution(mesh):
    placed = (P("cell", "aux", None, None), P(), P(), P("cell", None, None, "aux"), P())
    return jax.shard_map(
        on_device,
        mesh=mesh,
        in_specs=placed,
        out_specs=P(None, "aux", None, "cell"),
        check_vma=False,
    )
```

time: 197 us -> 72.7 us (0.37)
  the two profiles are of different devices: /device:TPU:1 before, /device:TPU:14 now
where the time goes in v1:
time: 72.7 us; the launch traced here: 72.4 us
  Pallas kernels  67.6 us (93%)
  local copies, waits for them, and re-layouts  2.59 us (4%)
  other arithmetic  2.24 us (3%)
    pallas_call x1, Pallas kernels, exchange(): pl.pallas_call(kernel, out_shape=jax.ShapeDtypeStruct((CELLS, 8, 2 * LANE...  67.6 us
    gather x1, local copies, waits for them, and re-layouts, on_device(): ordered = jnp.take(got, source, axis=0)[:, :, :PAIRS]  1.64 us

profile of v1, /device:TPU:14, one launch (start us, length us, event | category | flops | bytes accessed | tf_op | source)
XLA Modules:
  0.0 72.4 jit_solution(8299371221184638794)
XLA Ops:
  0.0 0.8 %select_reduce_fusion.1 = s32[64]{0:T(128)S(1)} fusion(s32[64]{0:T(128)} %param.9), kind=kLoop, calls=%fused_computation.4 | loop fusion | flops 12224 | bytes 512 | tf_op jit(solution)/shard_map/reduce_sum | solution.py:376
  0.8 0.7 broadcast_and_fusion
  1.5 0.6 select_reduce_fusion.pos
  2.1 67.6 %transform.1 = f32[64,8,256]{2,1,0:T(8,128)} custom-call(s32[64]{0:T(128)} %select_reduce_fusion.pos, f32[300,4,300]{2,1,0:T(4,128)} %bitcast.16, f32[60,2,300]{2,1,0:T(2,128)} %bitcast.17, f32[30,2,300]{2,1,0:T(2,128)} %bitcast.18), custom_call_target="tpu_custom_call" | custom-call | tf_op jit(solution)/shard_map/transform/pallas_call | solution.py:325
  69.7 1.6 %gather_fusion = f32[64,8,256]{2,1,0:T(8,128)S(1)} fusion(f32[64,8,256]{2,1,0:T(8,128)} %transform.1, s32[1024]{0:T(1024)S(1)} %pad_clamp_fusion), kind=kCustom, calls=%fused_computation | custom fusion | bytes 1048832 | tf_op jit(solution)/shard_map/jit(_take)/gather | solution.py:389
  71.3 0.1 slice_select_fusion
  71.5 1.0 %copy.8 = f32[64,8,225]{2,0,1:T(8,128)} copy(f32[64,8,225]{2,1,0:T(8,128)S(1)} %slice_select_fusion) | data formatting | bytes 921600 | tf_op jit(solution)/shard_map/reshape | solution.py:390
  (4 shorter events, 0.0 us)

commit v2 on v1

v2 whole, which is shorter than its diff:
```python
import functools

import jax
import jax.numpy as jnp
from jax import lax
from jax.experimental import pallas as pl
from jax.experimental.pallas import tpu as pltpu
from jax.sharding import PartitionSpec as P

CELLS = 64
AUX = 8
NB = 300
NO = 60
NV = 240
PIECE = NV // AUX
ROWS = 4
LANES = 128
WIDE = 2 * LANES
REST = NB - WIDE
HALF = LANES // 2
GROUP = 16
WORKERS = 60
PAIRS = 225
SLOTS = 64
FIRST, SMALL, SECOND = 0, 1, 2
MESH = pl.DeviceIdType.MESH
F32 = jnp.float32
BF16 = jnp.bfloat16


def split(x):
    high = x.astype(BF16)
    low = (x - high.astype(F32)).astype(BF16)
    return high, low


def dot(a, b, transposed=False):
    dims = (((1,), (1 if transposed else 0,)), ((), ()))
    return lax.dot_general(a, b, dims, preferred_element_type=F32)


def dot3(a, b, transposed=False):
    return (
        dot(a[0], b[0], transposed)
        + dot(a[0], b[1], transposed)
        + dot(a[1], b[0], transposed)
    )


def times_i(x, sign):
    return pltpu.roll(x, ROWS, 0) * sign


def four_points(x, sign):
    even, odd = x[0] + x[2], x[1] + x[3]
    left, right = x[0] - x[2], times_i(x[1] - x[3], sign)
    return even + odd, left + right, even - odd, left - right


def four_complex(x):
    def add(a, b):
        return a[0] + b[0], a[1] + b[1]

    def sub(a, b):
        return a[0] - b[0], a[1] - b[1]

    even, odd = add(x[0], x[2]), add(x[1], x[3])
    left, across = sub(x[0], x[2]), sub(x[1], x[3])
    return (
        add(even, odd),
        (left[0] - across[1], left[1] + across[0]),
        sub(even, odd),
        (left[0] + across[1], left[1] - across[0]),
    )


def wait_bytes(ref, sem):
    pltpu.make_async_copy(ref, ref, sem).wait()


def kernel(
    cells, blocks, occ, vir, out_0, out_1,
    cells_v, occ_v, blocks_v, pos_v, pos_s,
    sent_half_0, sent_half_1, sent_rest, got_half_0, got_half_1, got_rest,
    middle, middle_rest, sent_spec, sent_spec_rest, got_spec_0, got_spec_1, got_spec_rest,
    vir_own, vir_all, vir_rows, vir_high, vir_low, rest_high, rest_low, band, sent_pairs,
    load_sem, pos_sem, half_send, half_recv, half_local, spec_send, spec_recv, spec_local,
    pair_send, pair_recv, pair_local, vir_load_sem, vir_send, vir_recv, vir_local,
):
    me = lax.axis_index("cell")
    my_aux = lax.axis_index("aux")
    partner = my_aux + 1 - 2 * lax.rem(my_aux, 2)
    active = lax.rem(me, GROUP) != GROUP - 1
    my_slot = me - me // GROUP
    out = (out_0, out_1)
    sent_half = (sent_half_0, sent_rest, sent_half_1)
    got_half = (got_half_0, got_rest, got_half_1)
    got_spec = (got_spec_0, got_spec_rest, got_spec_1)

    barrier = pltpu.get_barrier_semaphore()

    def greet(j, carry):
        pl.semaphore_signal(
            barrier, inc=1, device_id={"cell": lax.rem(me + j, CELLS)}, device_id_type=MESH
        )
        return carry

    def greet_aux(j, carry):
        pl.semaphore_signal(
            barrier, inc=1, device_id={"aux": lax.rem(my_aux + 2 * j, AUX)}, device_id_type=MESH
        )
        return carry

    lax.fori_loop(1, CELLS, greet, 0)
    lax.fori_loop(1, AUX // 2, greet_aux, 0)
    pl.semaphore_signal(barrier, inc=1, device_id={"aux": partner}, device_id_type=MESH)

    occ_loads = [pltpu.make_async_copy(occ.at[:, t, :], occ_v.at[t], load_sem.at[t]) for t in range(2)]
    block_loads = [pltpu.make_async_copy(blocks.at[:, p, :], blocks_v.at[p], load_sem.at[2 + p]) for p in range(ROWS)]
    vir_load = pltpu.make_async_copy(vir, vir_own, vir_load_sem)
    cells_load = pltpu.make_async_copy(cells, cells_v, pos_sem)
    cells_load.start()
    for load in occ_loads + block_loads:
        load.start()
    vir_load.start()
    cells_load.wait()

    folded = cells_v[...] & 3
    number = folded[0:1] * 16 + folded[1:2] * 4 + folded[2:3]
    wanted = lax.broadcasted_iota(jnp.int32, (CELLS, CELLS), 0)
    holder = lax.broadcasted_iota(jnp.int32, (CELLS, CELLS), 1)
    found = jnp.sum(jnp.where(number == wanted, holder, 0), axis=1, keepdims=True)
    pos_v[...] = jnp.broadcast_to(found & (CELLS - 1), (CELLS, LANES))
    pos_copy = pltpu.make_async_copy(pos_v, pos_s, pos_sem)
    pos_copy.start()

    for load in occ_loads:
        load.wait()
    blank = jnp.zeros((SLOTS - NO, NB), F32)
    left = split(jnp.concatenate([occ_v[0], blank, -occ_v[1], blank], axis=0))

    def half_product(pair):
        for p in (2 * pair, 2 * pair + 1):
            block_loads[p].wait()
        for at in range(2):
            product = dot3(left, split(blocks_v[2 * pair + at, :, 0:WIDE]))
            for t in range(2):
                for n in range(2):
                    rows = product[t * SLOTS : t * SLOTS + NO, n * LANES : (n + 1) * LANES]
                    sent_half[2 * pair][pl.ds(t * 4 + n * 2 + at, NO, stride=8), :] = rows

    def rest_product():
        gap = jnp.zeros((NB, HALF - REST), F32)
        parts = []
        for at in range(2):
            for pair in range(2):
                parts += [blocks_v[2 * pair + at, :, WIDE:NB], gap]
        product = dot3(left, split(jnp.concatenate(parts, axis=1)))
        for t in range(2):
            for at in range(2):
                sent_rest[:, t * 2 + at, :] = product[t * SLOTS : t * SLOTS + NO, at * LANES : (at + 1) * LANES]

    def half_source(part, slot):
        if part == SMALL:
            return sent_rest.at[slot]
        return sent_half[part].at[pl.ds(pl.multiple_of(slot * 8, 8), 8)]

    def send_half(part):
        def one(j, carry):
            peer = lax.rem(me + j, CELLS)

            @pl.when(lax.rem(peer, GROUP) != GROUP - 1)
            def _():
                pltpu.make_async_remote_copy(
                    src_ref=half_source(part, peer - peer // GROUP),
                    dst_ref=got_half[part].at[me],
                    send_sem=half_send.at[part],
                    recv_sem=half_recv.at[part],
                    device_id={"cell": peer},
                    device_id_type=MESH,
                ).start()

            return carry

        lax.fori_loop(1, CELLS, one, 0)

        @pl.when(active)
        def _():
            pltpu.make_async_copy(half_source(part, my_slot), got_half[part].at[me], half_local.at[part]).start()

    half_product(0)
    pl.semaphore_wait(barrier, CELLS - 1 + AUX // 2)
    send_half(FIRST)

    def vir_slot(aux):
        return vir_all.at[pl.ds(aux * PIECE, PIECE)]

    def vir_copy(source, aux, target, sem):
        return pltpu.make_async_remote_copy(
            src_ref=source,
            dst_ref=vir_slot(aux),
            send_sem=vir_send.at[sem],
            recv_sem=vir_recv.at[sem],
            device_id={"aux": target},
            device_id_type=MESH,
        )

    vir_load.wait()

    def send_vir(j, carry):
        vir_copy(vir_own, my_aux, lax.rem(my_aux + 2 * j, AUX), 0).start()
        return carry

    lax.fori_loop(1, AUX // 2, send_vir, 0)
    vir_copy(vir_own, my_aux, partner, 1).start()
    own_vir = pltpu.make_async_copy(vir_own, vir_slot(my_aux), vir_local)
    own_vir.start()

    half_product(1)
    rest_product()
    send_half(SMALL)
    send_half(SECOND)

    pos_copy.wait()
    sign = jnp.where(lax.broadcasted_iota(jnp.int32, (8, LANES), 0) < ROWS, -1.0, 1.0).astype(F32)

    def spec_target(part):
        if part == SMALL:
            return got_spec_rest.at[my_slot]
        return got_spec[part].at[pl.ds(pl.multiple_of(my_slot * 8, 8), 8)]

    def spec_source(part, peer):
        if part == SMALL:
            return sent_spec_rest.at[peer]
        return sent_spec.at[part // 2, peer]

    def arrived_half(part):
        wait_bytes(got_half[part].at[pl.ds(0, CELLS - 1)], half_recv.at[part])
        wait_bytes(got_half[part].at[0], half_local.at[part])

    def send_spec(part):
        def one(j, carry):
            peer = lax.rem(me + j, CELLS)
            pltpu.make_async_remote_copy(
                src_ref=spec_source(part, peer),
                dst_ref=spec_target(part),
                send_sem=spec_send.at[part],
                recv_sem=spec_recv.at[part],
                device_id={"cell": peer},
                device_id_type=MESH,
            ).start()
            return carry

        lax.fori_loop(1, CELLS, one, 0)
        pltpu.make_async_copy(spec_source(part, me), spec_target(part), spec_local.at[part]).start()

    def fourier(part):
        arrived_half(part)
        for c in range(4):
            x = [[got_half[part][pos_s[a * 16 + b * 4 + c, 0]] for b in range(4)] for a in range(4)]
            columns = [four_points([x[a][b] for a in range(4)], sign) for b in range(4)]
            for a in range(4):
                y = four_points([columns[b][a] for b in range(4)], sign)
                for b in range(4):
                    middle[a * 16 + b * 4 + c] = y[b]
        for at in range(16):
            y = four_points([middle[at * 4 + c] for c in range(4)], sign)
            for c in range(4):
                sent_spec[part // 2, at * 4 + c] = y[c]
        send_spec(part)

    def fourier_rest():
        arrived_half(SMALL)
        for c in range(4):
            x = [[None] * 4 for _ in range(4)]
            for a in range(4):
                for b in range(4):
                    both = got_rest[pos_s[a * 16 + b * 4 + c, 0]]
                    x[a][b] = (both[0:2], both[2:4])
            columns = [four_complex([x[a][b] for a in range(4)]) for b in range(4)]
            for a in range(4):
                y = four_complex([columns[b][a] for b in range(4)])
                for b in range(4):
                    for t in range(2):
                        middle_rest[a * 16 + b * 4 + c, 2 * t : 2 * t + 2] = y[b][t]
        for at in range(16):
            x = [(middle_rest[at * 4 + c, 0:2], middle_rest[at * 4 + c, 2:4]) for c in range(4)]
            y = four_complex(x)
            for c in range(4):
                for t in range(2):
                    sent_spec_rest[at * 4 + c, 2 * t : 2 * t + 2] = y[c][t]
        send_spec(SMALL)

    @pl.when(active)
    def _():
        fourier(FIRST)

    wait_bytes(vir_all.at[pl.ds(0, NV // 2 - PIECE)], vir_recv.at[0])

    def hand_on(j, carry):
        source = lax.rem(my_aux + 2 * j, AUX)
        vir_copy(vir_slot(source), source, partner, 1).start()
        return carry

    lax.fori_loop(1, AUX // 2, hand_on, 0)

    @pl.when(active)
    def _():
        fourier_rest()
        fourier(SECOND)

    own_vir.wait()
    wait_bytes(vir_all.at[pl.ds(0, NV // 2)], vir_recv.at[1])
    spread = [pltpu.make_async_copy(vir_all.at[:, t, :], vir_rows.at[t], load_sem.at[t]) for t in range(2)]
    for copy in spread:
        copy.start()
    for copy in spread:
        copy.wait()
    gap = jnp.zeros((NV, HALF - REST), F32)
    none = jnp.zeros((NV, HALF), F32)
    for t in range(2):
        high, low = split(vir_rows[t, :, 0:WIDE])
        vir_high[:, t * WIDE : (t + 1) * WIDE] = high
        vir_low[:, t * WIDE : (t + 1) * WIDE] = low
        small = jnp.concatenate([vir_rows[t, :, WIDE:NB], gap], axis=1)
        for g in range(2):
            placed = jnp.concatenate([none, small] if g else [small, none], axis=1)
            high, low = split(placed)
            rest_high[g, :, t * LANES : (t + 1) * LANES] = high
            rest_low[g, :, t * LANES : (t + 1) * LANES] = low

    def arrived_spec(part):
        step = 1 if part == SMALL else 8

        @pl.when(active)
        def _():
            wait_bytes(got_spec[part].at[pl.ds(0, (WORKERS - 1) * step)], spec_recv.at[part])
            wait_bytes(got_spec[part].at[pl.ds(0, step)], spec_local.at[part])

        @pl.when(jnp.logical_not(active))
        def _():
            wait_bytes(got_spec[part].at[pl.ds(0, WORKERS * step)], spec_recv.at[part])

    def turned(even, odd):
        upper = jnp.concatenate(even + [-x for x in odd], axis=1)
        lower = jnp.concatenate(odd + even, axis=1)
        return [upper, lower]

    lane = lax.broadcasted_iota(jnp.int32, (ROWS, WIDE), 1)

    def band_and_pairs(g):
        part = 2 * g
        arrived_spec(part)
        if g == 0:
            arrived_spec(SMALL)
        main, small = [], []
        for at in range(2):
            x = [[got_spec[part][pl.ds(t * 4 + n * 2 + at, SLOTS, stride=8), :] for n in range(2)] for t in range(2)]
            main += turned(x[0], x[1])
            y = [got_spec_rest[:, t * 2 + at, :] for t in range(2)]
            small += turned([y[0]], [y[1]])
        value = dot3(split(jnp.concatenate(main, axis=0)), (vir_high[...], vir_low[...]), transposed=True)
        value = value + dot3(split(jnp.concatenate(small, axis=0)), (rest_high[g], rest_low[g]), transposed=True)
        value = jnp.concatenate([value, jnp.zeros((4 * SLOTS, WIDE - NV), F32)], axis=1)
        for at in range(2):
            for t in range(2):
                start = (at * 2 + t) * SLOTS
                for n in range(2):
                    band[g, n, pl.ds(t * 2 + at, NO, stride=4), :] = value[start : start + NO, n * LANES : (n + 1) * LANES]

        def wide(i):
            return jnp.concatenate([band[g, n, 4 * i : 4 * i + 4, :] for n in range(2)], axis=1)

        for block in range(4):
            base = block * (GROUP - 1)
            for m in range(GROUP):
                shift = (NV - PAIRS) * m
                if m == 0:
                    chunk = wide(base)
                else:
                    chunk = pltpu.roll(wide(base + m - 1), WIDE - (NV - shift), 1)
                    if m < GROUP - 1:
                        chunk = jnp.where(lane < shift, chunk, pltpu.roll(wide(base + m), shift, 1))
                sent_pairs[g, block * GROUP + m] = chunk

            def one(m, inner):
                peer = block * GROUP + m

                @pl.when(peer != me)
                def _():
                    pltpu.make_async_remote_copy(
                        src_ref=sent_pairs.at[g, peer],
                        dst_ref=out[g].at[me],
                        send_sem=pair_send.at[g],
                        recv_sem=pair_recv.at[g],
                        device_id={"cell": peer},
                        device_id_type=MESH,
                    ).start()

                @pl.when(peer == me)
                def _():
                    pltpu.make_async_copy(sent_pairs.at[g, peer], out[g].at[peer], pair_local.at[g]).start()

                return inner

            lax.fori_loop(0, GROUP, one, 0)

    for g in range(2):
        band_and_pairs(g)

    for part in (FIRST, SMALL, SECOND):
        step = 1 if part == SMALL else 8
        spec = sent_spec_rest if part == SMALL else sent_spec.at[part // 2]

        @pl.when(active)
        def _():
            wait_bytes(sent_half[part].at[pl.ds(0, (WORKERS - 1) * step)], half_send.at[part])
            wait_bytes(spec.at[pl.ds(0, CELLS - 1)], spec_send.at[part])

        @pl.when(jnp.logical_not(active))
        def _():
            wait_bytes(sent_half[part].at[pl.ds(0, WORKERS * step)], half_send.at[part])

    wait_bytes(vir_all.at[pl.ds(0, NV // 2 - PIECE)], vir_send.at[0])
    wait_bytes(vir_all.at[pl.ds(0, NV // 2)], vir_send.at[1])
    for g in range(2):
        wait_bytes(sent_pairs.at[g, pl.ds(0, CELLS - 1)], pair_send.at[g])
        wait_bytes(out[g].at[0], pair_local.at[g])
        wait_bytes(out[g].at[pl.ds(0, CELLS - 1)], pair_recv.at[g])


def exchange(cells, blocks, occ, vir):
    dma = pltpu.SemaphoreType.DMA
    pairs = jax.ShapeDtypeStruct((CELLS, ROWS, WIDE), F32)
    tiles = pltpu.VMEM((CELLS, 8, LANES), F32)
    halves = pltpu.VMEM((SLOTS, 4, LANES), F32)
    return pl.pallas_call(
        kernel,
        out_shape=(pairs, pairs),
        in_specs=[
            pl.BlockSpec(memory_space=pl.ANY),
            pl.BlockSpec(memory_space=pl.ANY),
            pl.BlockSpec(memory_space=pl.ANY),
            pl.BlockSpec(memory_space=pl.ANY),
        ],
        out_specs=(pl.BlockSpec(memory_space=pltpu.VMEM), pl.BlockSpec(memory_space=pltpu.VMEM)),
        scratch_shapes=[
            pltpu.VMEM((3, CELLS), jnp.int32),
            pltpu.VMEM((2, NO, NB), F32),
            pltpu.VMEM((ROWS, NB, NB), F32),
            pltpu.VMEM((CELLS, LANES), jnp.int32),
            pltpu.SMEM((CELLS, LANES), jnp.int32),
            pltpu.VMEM((WORKERS * 8, LANES), F32),
            pltpu.VMEM((WORKERS * 8, LANES), F32),
            pltpu.VMEM((WORKERS, 4, LANES), F32),
            tiles,
            tiles,
            halves,
            tiles,
            halves,
            pltpu.VMEM((2, CELLS, 8, LANES), F32),
            halves,
            pltpu.VMEM((SLOTS * 8, LANES), F32),
            pltpu.VMEM((SLOTS * 8, LANES), F32),
            halves,
            pltpu.VMEM((PIECE, 2, NB), F32),
            pltpu.VMEM((NV, 2, NB), F32),
            pltpu.VMEM((2, NV, NB), F32),
            pltpu.VMEM((NV, 2 * WIDE), BF16),
            pltpu.VMEM((NV, 2 * WIDE), BF16),
            pltpu.VMEM((2, NV, WIDE), BF16),
            pltpu.VMEM((2, NV, WIDE), BF16),
            pltpu.VMEM((2, 2, NO * 4, LANES), F32),
            pltpu.VMEM((2, CELLS, ROWS, WIDE), F32),
            dma((2 + ROWS,)),
            dma,
            dma((3,)),
            dma((3,)),
            dma((3,)),
            dma((3,)),
            dma((3,)),
            dma((3,)),
            dma((2,)),
            dma((2,)),
            dma((2,)),
            dma,
            dma((2,)),
            dma((2,)),
            dma,
        ],
        compiler_params=pltpu.CompilerParams(
            collective_id=0, has_side_effects=True, vmem_limit_bytes=44 << 20
        ),
        name="transform",
    )(cells, blocks, occ, vir)


def reorder_kernel(transfer, got_0, got_1, out, rows, ordered, sem):
    first = transfer[0]
    shifts = (first // 16, first // 4 % 4, first % 4)
    along = [[(n - shift) & 3 for n in range(4)] for shift in shifts]
    copies = []
    for g, got in enumerate((got_0, got_1)):
        for q in range(CELLS):
            source = along[0][q // 16] * 16 + along[1][q // 4 % 4] * 4 + along[2][q % 4]
            tile = got[source]
            for t in range(2):
                for n in range(2):
                    at = (t * ROWS + 2 * g) * CELLS + q
                    rows[n, pl.ds(at, 2, stride=CELLS), :] = tile[2 * t : 2 * t + 2, n * LANES : (n + 1) * LANES]
        for t in range(2):
            for p in (2 * g, 2 * g + 1):
                at = (t * ROWS + p) * CELLS
                ordered[t, p, :, 0:LANES] = rows[0, at : at + CELLS, :]
                ordered[t, p, :, LANES:PAIRS] = rows[1, at : at + CELLS, 0 : PAIRS - LANES]
            both = pl.ds(2 * g, 2)
            copy = pltpu.make_async_copy(ordered.at[t, both], out.at[t, both], sem.at[g, t])
            copy.start()
            copies.append(copy)
    for copy in copies:
        copy.wait()


def reorder(transfer, got_0, got_1):
    whole = pl.BlockSpec(memory_space=pltpu.VMEM)
    return pl.pallas_call(
        reorder_kernel,
        out_shape=jax.ShapeDtypeStruct((2, ROWS, CELLS, PAIRS), F32),
        in_specs=[pl.BlockSpec(memory_space=pltpu.SMEM), whole, whole],
        out_specs=pl.BlockSpec(memory_space=pl.ANY),
        scratch_shapes=[
            pltpu.VMEM((2, 2 * ROWS * CELLS, LANES), F32),
            pltpu.VMEM((2, ROWS, CELLS, PAIRS), F32),
            pltpu.SemaphoreType.DMA((2, 2)),
        ],
        compiler_params=pltpu.CompilerParams(vmem_limit_bytes=16 << 20),
        name="reorder",
    )(transfer, got_0, got_1)


def on_device(blocks, cell_offsets, occ_coeff, vir_coeff, transfer_index):
    keep = functools.partial(pltpu.with_memory_space_constraint, memory_space=pltpu.HBM)
    got = exchange(
        keep(cell_offsets),
        keep(jnp.transpose(blocks[0], (1, 0, 2))),
        keep(jnp.transpose(occ_coeff, (2, 0, 1))),
        keep(jnp.transpose(vir_coeff[0], (2, 0, 1))),
    )
    return reorder(transfer_index, *got)


def solution(mesh):
    placed = (P("cell", "aux", None, None), P(), P(), P("cell", None, None, "aux"), P())
    return jax.shard_map(
        on_device,
        mesh=mesh,
        in_specs=placed,
        out_specs=P(None, "aux", None, "cell"),
        check_vma=False,
    )
```

time: 72.7 us -> 62 us (0.85)
  the two profiles are of different devices: /device:TPU:14 before, /device:TPU:1 now
where the time goes in v2:
time: 62 us; the launch traced here: 61.1 us
  Pallas kernels  61.1 us (99%)
    pallas_call x1, Pallas kernels, exchange(): pl.pallas_call(kernel, out_shape=(pairs, pairs), in_specs=[pl.BlockSpec(m...  59.5 us
    pallas_call x1, Pallas kernels, reorder(): pl.pallas_call(reorder_kernel, out_shape=jax.ShapeDtypeStruct((2, ROWS, C...  1.65 us

profile of v2, /device:TPU:1, one launch (start us, length us, event | category | flops | bytes accessed | tf_op | source)
XLA Modules:
  0.0 61.1 jit_solution(8989188839120418070)
XLA Ops:
  0.0 0.0 copy-start
  0.0 59.5 %transform.1 = (f32[64,4,256]{2,1,0:T(4,128)S(1)}, f32[64,4,256]{2,1,0:T(4,128)S(1)}) custom-call(s32[3,64]{1,0:T(4,128)} %cells.1, f32[300,4,300]{2,1,0:T(4,128)} %bitcast.7, f32[60,2,300]{2,1,0:T(2,128)} %bitcast.8, f32[30,2,300]{2,1,0:T(2,128)} %bitcast.9), custom_call_target="tpu_custom_call" | custom-call | tf_op jit(solution)/shard_map/transform/pallas_call | solution.py:437
  59.5 0.0 copy-done
  59.5 1.7 %reorder.1 = f32[2,4,64,225]{3,2,1,0:T(8,128)} custom-call(s32[64]{0:T(128)S(1)} %copy-done, f32[64,4,256]{2,1,0:T(4,128)S(1)} %get-tuple-element.7.got_0, f32[64,4,256]{2,1,0:T(4,128)S(1)} %get-tuple-element.8.got_1), custom_call_target="tpu_custom_call" | custom-call | tf_op jit(solution)/shard_map/reorder/pallas_call | solution.py:526
Async XLA Ops:
  0.0 59.5 %copy-start = (s32[64]{0:T(128)S(1)}, s32[64]{0:T(128)}, u32[]{:S(2)}) copy-start(s32[64]{0:T(128)} %transfer.1) | copy-start | bytes 772

commit v3 on v2

--- a/solution.py
+++ b/solution.py
@@ -18,10 +18,13 @@
 WIDE = 2 * LANES
 REST = NB - WIDE
 HALF = LANES // 2
+STRIPS = 5
 GROUP = 16
 WORKERS = 60
 PAIRS = 225
 SLOTS = 64
+SIDE = CELLS // 2
+SHARE = WORKERS // 2
 FIRST, SMALL, SECOND = 0, 1, 2
 MESH = pl.DeviceIdType.MESH
 F32 = jnp.float32
@@ -82,8 +85,8 @@
     cells, blocks, occ, vir, out_0, out_1,
     cells_v, occ_v, blocks_v, pos_v, pos_s,
     sent_half_0, sent_half_1, sent_rest, got_half_0, got_half_1, got_rest,
-    middle, middle_rest, sent_spec, sent_spec_rest, got_spec_0, got_spec_1, got_spec_rest,
-    vir_own, vir_all, vir_rows, vir_high, vir_low, rest_high, rest_low, band, sent_pairs,
+    middle, middle_rest, whole_rest, sent_spec, sent_spec_rest, got_spec_0, got_spec_1, got_rest_0, got_rest_1,
+    vir_own, vir_sent, vir_all, vir_high, vir_low, rest_high, rest_low, band, sent_pairs,
     load_sem, pos_sem, half_send, half_recv, half_local, spec_send, spec_recv, spec_local,
     pair_send, pair_recv, pair_local, vir_load_sem, vir_send, vir_recv, vir_local,
 ):
@@ -95,13 +98,27 @@
     out = (out_0, out_1)
     sent_half = (sent_half_0, sent_rest, sent_half_1)
     got_half = (got_half_0, got_rest, got_half_1)
-    got_spec = (got_spec_0, got_spec_rest, got_spec_1)
+    got_spec = (got_spec_0, got_spec_1)
+    got_spec_rest = (got_rest_0, got_rest_1)
+    my_low, my_side = lax.rem(me, SIDE), me // SIDE
+
+    def member(g, j):
+        start = GROUP * g
+        at = lax.rem(me + CELLS - start, CELLS)
+        u = lax.rem(at + SIDE // 2 + (j + 1) // 2 * (1 - 2 * lax.rem(j, 2)), SIDE)
+        return lax.rem(start + at // SIDE * SIDE + u, CELLS), u
+
+    def share_slot(g):
+        return lax.rem(my_slot + WORKERS - (GROUP - 1) * g, SHARE)
+
+    def far_first(j):
+        return lax.rem(me + CELLS // 2 + (j + 1) // 2 * (1 - 2 * lax.rem(j, 2)), CELLS)
 
     barrier = pltpu.get_barrier_semaphore()
 
     def greet(j, carry):
         pl.semaphore_signal(
-            barrier, inc=1, device_id={"cell": lax.rem(me + j, CELLS)}, device_id_type=MESH
+            barrier, inc=1, device_id={"cell": far_first(j)}, device_id_type=MESH
         )
         return carry
 
@@ -111,7 +128,7 @@
         )
         return carry
 
-    lax.fori_loop(1, CELLS, greet, 0)
+    lax.fori_loop(0, CELLS - 1, greet, 0)
     lax.fori_loop(1, AUX // 2, greet_aux, 0)
     pl.semaphore_signal(barrier, inc=1, device_id={"aux": partner}, device_id_type=MESH)
 
@@ -120,9 +137,9 @@
     vir_load = pltpu.make_async_copy(vir, vir_own, vir_load_sem)
     cells_load = pltpu.make_async_copy(cells, cells_v, pos_sem)
     cells_load.start()
+    vir_load.start()
     for load in occ_loads + block_loads:
         load.start()
-    vir_load.start()
     cells_load.wait()
 
     folded = cells_v[...] & 3
@@ -134,14 +151,49 @@
     pos_copy = pltpu.make_async_copy(pos_v, pos_s, pos_sem)
     pos_copy.start()
 
+    def vir_slot(side, aux):
+        return vir_all.at[side, :, pl.ds(aux * PIECE, PIECE)]
+
+    def vir_copy(source, side, aux, target, sem):
+        return pltpu.make_async_remote_copy(
+            src_ref=source,
+            dst_ref=vir_slot(side, aux),
+            send_sem=vir_send.at[sem],
+            recv_sem=vir_recv.at[sem],
+            device_id=target,
+            device_id_type=MESH,
+        )
+
+    def spread_vir(source, side):
+        def one(j, carry):
+            vir_copy(source, side, my_aux, {"aux": lax.rem(my_aux + 2 * j, AUX)}, 0).start()
+            return carry
+
+        lax.fori_loop(1, AUX // 2, one, 0)
+        vir_copy(source, side, my_aux, {"aux": partner}, 1).start()
+
+    vir_load.wait()
+    shut = jnp.zeros((PIECE, HALF - REST), F32)
+    for t in range(2):
+        for n in range(2):
+            vir_sent[n * 2 + t, :, 0, :] = vir_own[:, t, n * LANES : (n + 1) * LANES]
+    vir_sent[STRIPS - 1, :, 0, :] = jnp.concatenate(
+        [vir_own[:, 0, WIDE:NB], shut, vir_own[:, 1, WIDE:NB], shut], axis=1
+    )
+    pl.semaphore_wait(barrier, CELLS - 1 + AUX // 2)
+    vir_copy(vir_sent, my_side, my_aux, {"cell": lax.rem(me + SIDE, CELLS)}, 2).start()
+    spread_vir(vir_sent, my_side)
+    own_vir = pltpu.make_async_copy(vir_sent, vir_slot(my_side, my_aux), vir_local)
+    own_vir.start()
+
     for load in occ_loads:
         load.wait()
     blank = jnp.zeros((SLOTS - NO, NB), F32)
     left = split(jnp.concatenate([occ_v[0], blank, -occ_v[1], blank], axis=0))
 
     def half_product(pair):
-        for p in (2 * pair, 2 * pair + 1):
-            block_loads[p].wait()
+        for load in block_loads[2 * pair : 2 * pair + 2]:
+            load.wait()
         for at in range(2):
             product = dot3(left, split(blocks_v[2 * pair + at, :, 0:WIDE]))
             for t in range(2):
@@ -167,7 +219,7 @@
 
     def send_half(part):
         def one(j, carry):
-            peer = lax.rem(me + j, CELLS)
+            peer = far_first(j)
 
             @pl.when(lax.rem(peer, GROUP) != GROUP - 1)
             def _():
@@ -182,39 +234,14 @@
 
             return carry
 
-        lax.fori_loop(1, CELLS, one, 0)
+        lax.fori_loop(0, CELLS - 1, one, 0)
 
         @pl.when(active)
         def _():
             pltpu.make_async_copy(half_source(part, my_slot), got_half[part].at[me], half_local.at[part]).start()
 
     half_product(0)
-    pl.semaphore_wait(barrier, CELLS - 1 + AUX // 2)
     send_half(FIRST)
-
-    def vir_slot(aux):
-        return vir_all.at[pl.ds(aux * PIECE, PIECE)]
-
-    def vir_copy(source, aux, target, sem):
-        return pltpu.make_async_remote_copy(
-            src_ref=source,
-            dst_ref=vir_slot(aux),
-            send_sem=vir_send.at[sem],
-            recv_sem=vir_recv.at[sem],
-            device_id={"aux": target},
-            device_id_type=MESH,
-        )
-
-    vir_load.wait()
-
-    def send_vir(j, carry):
-        vir_copy(vir_own, my_aux, lax.rem(my_aux + 2 * j, AUX), 0).start()
-        return carry
-
-    lax.fori_loop(1, AUX // 2, send_vir, 0)
-    vir_copy(vir_own, my_aux, partner, 1).start()
-    own_vir = pltpu.make_async_copy(vir_own, vir_slot(my_aux), vir_local)
-    own_vir.start()
 
     half_product(1)
     rest_product()
@@ -222,37 +249,35 @@
     send_half(SECOND)
 
     pos_copy.wait()
+    first_half = lax.broadcasted_iota(jnp.int32, (2, LANES), 1) < HALF
     sign = jnp.where(lax.broadcasted_iota(jnp.int32, (8, LANES), 0) < ROWS, -1.0, 1.0).astype(F32)
 
-    def spec_target(part):
+    def spec_copy(part, g):
         if part == SMALL:
-            return got_spec_rest.at[my_slot]
-        return got_spec[part].at[pl.ds(pl.multiple_of(my_slot * 8, 8), 8)]
-
-    def spec_source(part, peer):
-        if part == SMALL:
-            return sent_spec_rest.at[peer]
-        return sent_spec.at[part // 2, peer]
+            return sent_spec_rest.at[g], got_spec_rest[g].at[share_slot(g)], 2 + g
+        return sent_spec.at[g], got_spec[g].at[:, pl.ds(pl.multiple_of(share_slot(g) * 8, 8), 8)], g
 
     def arrived_half(part):
         wait_bytes(got_half[part].at[pl.ds(0, CELLS - 1)], half_recv.at[part])
         wait_bytes(got_half[part].at[0], half_local.at[part])
 
-    def send_spec(part):
+    def send_spec(part, g):
+        sources, target, sem = spec_copy(part, g)
+
         def one(j, carry):
-            peer = lax.rem(me + j, CELLS)
+            peer, _ = member(g, j)
             pltpu.make_async_remote_copy(
-                src_ref=spec_source(part, peer),
-                dst_ref=spec_target(part),
-                send_sem=spec_send.at[part],
-                recv_sem=spec_recv.at[part],
+                src_ref=sources.at[lax.rem(peer, SIDE)],
+                dst_ref=target,
+                send_sem=spec_send.at[sem],
+                recv_sem=spec_recv.at[sem],
                 device_id={"cell": peer},
                 device_id_type=MESH,
             ).start()
             return carry
 
-        lax.fori_loop(1, CELLS, one, 0)
-        pltpu.make_async_copy(spec_source(part, me), spec_target(part), spec_local.at[part]).start()
+        lax.fori_loop(0, SIDE - 1, one, 0)
+        pltpu.make_async_copy(sources.at[my_low], target, spec_local.at[sem]).start()
 
     def fourier(part):
         arrived_half(part)
@@ -266,8 +291,9 @@
         for at in range(16):
             y = four_points([middle[at * 4 + c] for c in range(4)], sign)
             for c in range(4):
-                sent_spec[part // 2, at * 4 + c] = y[c]
-        send_spec(part)
+                k = at * 4 + c
+                sent_spec[part // 2, k % SIDE, k // SIDE] = y[c]
+        send_spec(part, part // 2)
 
     def fourier_rest():
         arrived_half(SMALL)
@@ -288,58 +314,67 @@
             y = four_complex(x)
             for c in range(4):
                 for t in range(2):
-                    sent_spec_rest[at * 4 + c, 2 * t : 2 * t + 2] = y[c][t]
-        send_spec(SMALL)
+                    whole_rest[at * 4 + c, 2 * t : 2 * t + 2] = y[c][t]
+        for k in range(SIDE):
+            for t in range(2):
+                rows = slice(2 * t, 2 * t + 2)
+                low, high = whole_rest[k, rows], whole_rest[k + SIDE, rows]
+                sent_spec_rest[0, k, rows] = jnp.where(first_half, low, pltpu.roll(high, HALF, 1))
+                sent_spec_rest[1, k, rows] = jnp.where(first_half, pltpu.roll(low, HALF, 1), high)
+        for g in range(2):
+            send_spec(SMALL, g)
+
+    other = 1 - my_side
+    wait_bytes(vir_slot(0, 0), vir_recv.at[2])
+    spread_vir(vir_slot(other, my_aux), other)
 
     @pl.when(active)
     def _():
         fourier(FIRST)
-
-    wait_bytes(vir_all.at[pl.ds(0, NV // 2 - PIECE)], vir_recv.at[0])
+        fourier_rest()
+        fourier(SECOND)
+
+    wait_bytes(vir_all.at[:, :, pl.ds(0, NV // 2 - PIECE)], vir_recv.at[0])
 
     def hand_on(j, carry):
         source = lax.rem(my_aux + 2 * j, AUX)
-        vir_copy(vir_slot(source), source, partner, 1).start()
+        for side in range(2):
+            vir_copy(vir_slot(side, source), side, source, {"aux": partner}, 1).start()
         return carry
 
     lax.fori_loop(1, AUX // 2, hand_on, 0)
-
-    @pl.when(active)
-    def _():
-        fourier_rest()
-        fourier(SECOND)
-
     own_vir.wait()
-    wait_bytes(vir_all.at[pl.ds(0, NV // 2)], vir_recv.at[1])
-    spread = [pltpu.make_async_copy(vir_all.at[:, t, :], vir_rows.at[t], load_sem.at[t]) for t in range(2)]
-    for copy in spread:
-        copy.start()
-    for copy in spread:
-        copy.wait()
-    gap = jnp.zeros((NV, HALF - REST), F32)
+    wait_bytes(vir_all.at[:, :, pl.ds(0, NV // 2)], vir_recv.at[1])
     none = jnp.zeros((NV, HALF), F32)
-    for t in range(2):
-        high, low = split(vir_rows[t, :, 0:WIDE])
-        vir_high[:, t * WIDE : (t + 1) * WIDE] = high
-        vir_low[:, t * WIDE : (t + 1) * WIDE] = low
-        small = jnp.concatenate([vir_rows[t, :, WIDE:NB], gap], axis=1)
-        for g in range(2):
-            placed = jnp.concatenate([none, small] if g else [small, none], axis=1)
-            high, low = split(placed)
-            rest_high[g, :, t * LANES : (t + 1) * LANES] = high
-            rest_low[g, :, t * LANES : (t + 1) * LANES] = low
-
-    def arrived_spec(part):
-        step = 1 if part == SMALL else 8
+    for side in range(2):
+        rest = vir_all[side, STRIPS - 1, :, 0, :]
+        for t in range(2):
+            for n in range(2):
+                high, low = split(vir_all[side, n * 2 + t, :, 0, :])
+                at = t * WIDE + n * LANES
+                vir_high[side, :, at : at + LANES] = high
+                vir_low[side, :, at : at + LANES] = low
+            small = rest[:, t * HALF : (t + 1) * HALF]
+            high, low = split(jnp.concatenate([none, small] if side else [small, none], axis=1))
+            rest_high[side, :, t * LANES : (t + 1) * LANES] = high
+            rest_low[side, :, t * LANES : (t + 1) * LANES] = low
+
+    def spec_bytes(part, g, count):
+        if part == SMALL:
+            return got_spec_rest[g].at[pl.ds(0, count)]
+        return got_spec[g].at[:, pl.ds(0, count * 8)]
+
+    def arrived_spec(part, g):
+        sem = spec_copy(part, g)[2]
 
         @pl.when(active)
         def _():
-            wait_bytes(got_spec[part].at[pl.ds(0, (WORKERS - 1) * step)], spec_recv.at[part])
-            wait_bytes(got_spec[part].at[pl.ds(0, step)], spec_local.at[part])
+            wait_bytes(spec_bytes(part, g, SHARE - 1), spec_recv.at[sem])
+            wait_bytes(spec_bytes(part, g, 1), spec_local.at[sem])
 
         @pl.when(jnp.logical_not(active))
         def _():
-            wait_bytes(got_spec[part].at[pl.ds(0, WORKERS * step)], spec_recv.at[part])
+            wait_bytes(spec_bytes(part, g, SHARE), spec_recv.at[sem])
 
     def turned(even, odd):
         upper = jnp.concatenate(even + [-x for x in odd], axis=1)
@@ -349,89 +384,94 @@
     lane = lax.broadcasted_iota(jnp.int32, (ROWS, WIDE), 1)
 
     def band_and_pairs(g):
-        part = 2 * g
-        arrived_spec(part)
-        if g == 0:
-            arrived_spec(SMALL)
-        main, small = [], []
-        for at in range(2):
-            x = [[got_spec[part][pl.ds(t * 4 + n * 2 + at, SLOTS, stride=8), :] for n in range(2)] for t in range(2)]
-            main += turned(x[0], x[1])
-            y = [got_spec_rest[:, t * 2 + at, :] for t in range(2)]
-            small += turned([y[0]], [y[1]])
-        value = dot3(split(jnp.concatenate(main, axis=0)), (vir_high[...], vir_low[...]), transposed=True)
-        value = value + dot3(split(jnp.concatenate(small, axis=0)), (rest_high[g], rest_low[g]), transposed=True)
-        value = jnp.concatenate([value, jnp.zeros((4 * SLOTS, WIDE - NV), F32)], axis=1)
-        for at in range(2):
-            for t in range(2):
-                start = (at * 2 + t) * SLOTS
-                for n in range(2):
-                    band[g, n, pl.ds(t * 2 + at, NO, stride=4), :] = value[start : start + NO, n * LANES : (n + 1) * LANES]
-
-        def wide(i):
-            return jnp.concatenate([band[g, n, 4 * i : 4 * i + 4, :] for n in range(2)], axis=1)
-
-        for block in range(4):
+        arrived_spec(2 * g, g)
+        arrived_spec(SMALL, g)
+        for side in range(2):
+            main, small = [], []
+            for at in range(2):
+                x = [
+                    [got_spec[g][side, pl.ds(t * 4 + n * 2 + at, SIDE, stride=8), :] for n in range(2)]
+                    for t in range(2)
+                ]
+                main += turned(x[0], x[1])
+                y = [got_spec_rest[g][:, t * 2 + at, :] for t in range(2)]
+                small += turned([y[0]], [y[1]])
+            value = dot3(split(jnp.concatenate(main, axis=0)), (vir_high[side], vir_low[side]), transposed=True)
+            value = value + dot3(split(jnp.concatenate(small, axis=0)), (rest_high[side], rest_low[side]), transposed=True)
+            value = jnp.concatenate([value, jnp.zeros((4 * SIDE, WIDE - NV), F32)], axis=1)
+            for at in range(2):
+                for t in range(2):
+                    start = (at * 2 + t) * SIDE
+                    for n in range(2):
+                        band[g, side, n, pl.ds(t * 2 + at, SHARE, stride=4), :] = value[
+                            start : start + SHARE, n * LANES : (n + 1) * LANES
+                        ]
+
+        for block in range(2):
             base = block * (GROUP - 1)
-            for m in range(GROUP):
-                shift = (NV - PAIRS) * m
-                if m == 0:
-                    chunk = wide(base)
-                else:
-                    chunk = pltpu.roll(wide(base + m - 1), WIDE - (NV - shift), 1)
-                    if m < GROUP - 1:
-                        chunk = jnp.where(lane < shift, chunk, pltpu.roll(wide(base + m), shift, 1))
-                sent_pairs[g, block * GROUP + m] = chunk
-
-            def one(m, inner):
-                peer = block * GROUP + m
-
-                @pl.when(peer != me)
-                def _():
-                    pltpu.make_async_remote_copy(
-                        src_ref=sent_pairs.at[g, peer],
-                        dst_ref=out[g].at[me],
-                        send_sem=pair_send.at[g],
-                        recv_sem=pair_recv.at[g],
-                        device_id={"cell": peer},
-                        device_id_type=MESH,
-                    ).start()
-
-                @pl.when(peer == me)
-                def _():
-                    pltpu.make_async_copy(sent_pairs.at[g, peer], out[g].at[peer], pair_local.at[g]).start()
-
-                return inner
-
-            lax.fori_loop(0, GROUP, one, 0)
+            for side in range(2):
+
+                def wide(i):
+                    return jnp.concatenate([band[g, side, n, 4 * i : 4 * i + 4, :] for n in range(2)], axis=1)
+
+                for m in range(GROUP):
+                    shift = (NV - PAIRS) * m
+                    if m == 0:
+                        chunk = wide(base)
+                    else:
+                        chunk = pltpu.roll(wide(base + m - 1), WIDE - (NV - shift), 1)
+                        if m < GROUP - 1:
+                            chunk = jnp.where(lane < shift, chunk, pltpu.roll(wide(base + m), shift, 1))
+                    sent_pairs[g, block * GROUP + m, side] = chunk
+
+        def one(j, carry):
+            peer, u = member(g, j)
+            pltpu.make_async_remote_copy(
+                src_ref=sent_pairs.at[g, u],
+                dst_ref=out[g].at[my_low],
+                send_sem=pair_send.at[g],
+                recv_sem=pair_recv.at[g],
+                device_id={"cell": peer},
+                device_id_type=MESH,
+            ).start()
+            return carry
+
+        lax.fori_loop(0, SIDE - 1, one, 0)
+        my_place = lax.rem(me + CELLS - GROUP * g, SIDE)
+        pltpu.make_async_copy(sent_pairs.at[g, my_place], out[g].at[my_low], pair_local.at[g]).start()
 
     for g in range(2):
         band_and_pairs(g)
 
     for part in (FIRST, SMALL, SECOND):
         step = 1 if part == SMALL else 8
-        spec = sent_spec_rest if part == SMALL else sent_spec.at[part // 2]
 
         @pl.when(active)
         def _():
             wait_bytes(sent_half[part].at[pl.ds(0, (WORKERS - 1) * step)], half_send.at[part])
-            wait_bytes(spec.at[pl.ds(0, CELLS - 1)], spec_send.at[part])
 
         @pl.when(jnp.logical_not(active))
         def _():
             wait_bytes(sent_half[part].at[pl.ds(0, WORKERS * step)], half_send.at[part])
 
-    wait_bytes(vir_all.at[pl.ds(0, NV // 2 - PIECE)], vir_send.at[0])
-    wait_bytes(vir_all.at[pl.ds(0, NV // 2)], vir_send.at[1])
+    @pl.when(active)
+    def _():
+        for g in range(2):
+            wait_bytes(sent_spec.at[g, pl.ds(0, SIDE - 1)], spec_send.at[g])
+            wait_bytes(sent_spec_rest.at[g, pl.ds(0, SIDE - 1)], spec_send.at[2 + g])
+
+    wait_bytes(vir_all.at[:, :, pl.ds(0, NV // 2 - PIECE)], vir_send.at[0])
+    wait_bytes(vir_all.at[:, :, pl.ds(0, NV // 2)], vir_send.at[1])
+    wait_bytes(vir_slot(0, 0), vir_send.at[2])
     for g in range(2):
-        wait_bytes(sent_pairs.at[g, pl.ds(0, CELLS - 1)], pair_send.at[g])
+        wait_bytes(sent_pairs.at[g, pl.ds(0, SIDE - 1)], pair_send.at[g])
         wait_bytes(out[g].at[0], pair_local.at[g])
-        wait_bytes(out[g].at[pl.ds(0, CELLS - 1)], pair_recv.at[g])
+        wait_bytes(out[g].at[pl.ds(0, SIDE - 1)], pair_recv.at[g])
 
 
 def exchange(cells, blocks, occ, vir):
     dma = pltpu.SemaphoreType.DMA
-    pairs = jax.ShapeDtypeStruct((CELLS, ROWS, WIDE), F32)
+    pairs = jax.ShapeDtypeStruct((SIDE, 2, ROWS, WIDE), F32)
     tiles = pltpu.VMEM((CELLS, 8, LANES), F32)
     halves = pltpu.VMEM((SLOTS, 4, LANES), F32)
     return pl.pallas_call(
@@ -458,34 +498,36 @@
             halves,
             tiles,
             halves,
-            pltpu.VMEM((2, CELLS, 8, LANES), F32),
             halves,
-            pltpu.VMEM((SLOTS * 8, LANES), F32),
-            pltpu.VMEM((SLOTS * 8, LANES), F32),
-            halves,
+            pltpu.VMEM((2, SIDE, 2, 8, LANES), F32),
+            pltpu.VMEM((2, SIDE, 4, LANES), F32),
+            pltpu.VMEM((2, SIDE * 8, LANES), F32),
+            pltpu.VMEM((2, SIDE * 8, LANES), F32),
+            pltpu.VMEM((SIDE, 4, LANES), F32),
+            pltpu.VMEM((SIDE, 4, LANES), F32),
             pltpu.VMEM((PIECE, 2, NB), F32),
-            pltpu.VMEM((NV, 2, NB), F32),
-            pltpu.VMEM((2, NV, NB), F32),
-            pltpu.VMEM((NV, 2 * WIDE), BF16),
-            pltpu.VMEM((NV, 2 * WIDE), BF16),
+            pltpu.VMEM((STRIPS, PIECE, 1, LANES), F32),
+            pltpu.VMEM((2, STRIPS, NV, 1, LANES), F32),
+            pltpu.VMEM((2, NV, 2 * WIDE), BF16),
+            pltpu.VMEM((2, NV, 2 * WIDE), BF16),
             pltpu.VMEM((2, NV, WIDE), BF16),
             pltpu.VMEM((2, NV, WIDE), BF16),
-            pltpu.VMEM((2, 2, NO * 4, LANES), F32),
-            pltpu.VMEM((2, CELLS, ROWS, WIDE), F32),
+            pltpu.VMEM((2, 2, 2, SHARE * 4, LANES), F32),
+            pltpu.VMEM((2, SIDE, 2, ROWS, WIDE), F32),
             dma((2 + ROWS,)),
             dma,
             dma((3,)),
             dma((3,)),
             dma((3,)),
-            dma((3,)),
-            dma((3,)),
-            dma((3,)),
+            dma((4,)),
+            dma((4,)),
+            dma((4,)),
             dma((2,)),
             dma((2,)),
             dma((2,)),
             dma,
-            dma((2,)),
-            dma((2,)),
+            dma((3,)),
+            dma((3,)),
             dma,
         ],
         compiler_params=pltpu.CompilerParams(
@@ -503,7 +545,7 @@
     for g, got in enumerate((got_0, got_1)):
         for q in range(CELLS):
             source = along[0][q // 16] * 16 + along[1][q // 4 % 4] * 4 + along[2][q % 4]
-            tile = got[source]
+            tile = got[source & (SIDE - 1), source >> 5]
             for t in range(2):
                 for n in range(2):
                     at = (t * ROWS + 2 * g) * CELLS + q

time: 62 us -> 60.2 us (0.971); the launches traced: 61.1 us -> 60 us
  Pallas kernels: 61.1 us -> 60 us
    pallas_call x1, Pallas kernels: 59.5 us -> 58.3 us  [exchange(): pl.pallas_call(kernel, out_shape=(pairs, pairs), in_specs=[pl.BlockSpec(m...]
where the time goes in v3:
time: 60.2 us; the launch traced here: 60 us
  Pallas kernels  60 us (100%)
    pallas_call x1, Pallas kernels, exchange(): pl.pallas_call(kernel, out_shape=(pairs, pairs), in_specs=[pl.BlockSpec(m...  58.3 us
    pallas_call x1, Pallas kernels, reorder(): pl.pallas_call(reorder_kernel, out_shape=jax.ShapeDtypeStruct((2, ROWS, C...  1.72 us

profile of v3, /device:TPU:1, one launch (start us, length us, event | category | flops | bytes accessed | tf_op | source)
XLA Modules:
  0.0 60.0 jit_solution(9733445808425968399)
XLA Ops:
  0.0 0.0 copy-start
  0.0 58.3 %transform.1 = (f32[32,2,4,256]{3,2,1,0:T(4,128)S(1)}, f32[32,2,4,256]{3,2,1,0:T(4,128)S(1)}) custom-call(s32[3,64]{1,0:T(4,128)} %cells.1, f32[300,4,300]{2,1,0:T(4,128)} %bitcast.7, f32[60,2,300]{2,1,0:T(2,128)} %bitcast.8, f32[30,2,300]{2,1,0:T(2,128)} %bitcast.9), custom_call_target="tpu_custom_call" | custom-call | tf_op jit(solution)/shard_map/transform/pallas_call | solution.py:477
  58.3 0.0 copy-done
  58.3 1.7 %reorder.1 = f32[2,4,64,225]{3,2,1,0:T(8,128)} custom-call(s32[64]{0:T(128)S(1)} %copy-done, f32[32,2,4,256]{3,2,1,0:T(4,128)S(1)} %get-tuple-element.7.got_0, f32[32,2,4,256]{3,2,1,0:T(4,128)S(1)} %get-tuple-element.8.got_1), custom_call_target="tpu_custom_call" | custom-call | tf_op jit(solution)/shard_map/reorder/pallas_call | solution.py:568
Async XLA Ops:
  0.0 58.3 %copy-start = (s32[64]{0:T(128)S(1)}, s32[64]{0:T(128)}, u32[]{:S(2)}) copy-start(s32[64]{0:T(128)} %transfer.1) | copy-start | bytes 772

commit v4 on v3

--- a/solution.py
+++ b/solution.py
@@ -77,6 +77,10 @@
     )
 
 
+def wrapped(x, length):
+    return jnp.where(x >= length, x - length, x)
+
+
 def wait_bytes(ref, sem):
     pltpu.make_async_copy(ref, ref, sem).wait()
 
@@ -101,36 +105,29 @@
     got_spec = (got_spec_0, got_spec_1)
     got_spec_rest = (got_rest_0, got_rest_1)
     my_low, my_side = lax.rem(me, SIDE), me // SIDE
-
-    def member(g, j):
-        start = GROUP * g
-        at = lax.rem(me + CELLS - start, CELLS)
-        u = lax.rem(at + SIDE // 2 + (j + 1) // 2 * (1 - 2 * lax.rem(j, 2)), SIDE)
-        return lax.rem(start + at // SIDE * SIDE + u, CELLS), u
+    my_block = me // GROUP
+    my_first = wrapped(lax.rem(me, GROUP), GROUP - 1)
+    share_at, share_start = [], []
+    for g in range(2):
+        place = wrapped(me + CELLS - GROUP * g, CELLS)
+        share_at.append(lax.rem(place, SIDE))
+        share_start.append(GROUP * g + place // SIDE * SIDE)
+
+    def for_members(g, send):
+        def at(offset):
+            u = wrapped(share_at[g] + offset, SIDE)
+            send(wrapped(share_start[g] + u, CELLS), u)
+
+        def one(j, carry):
+            at(SIDE // 2 - j)
+            at(SIDE // 2 + j)
+            return carry
+
+        at(SIDE // 2)
+        lax.fori_loop(1, SIDE // 2, one, 0)
 
     def share_slot(g):
         return lax.rem(my_slot + WORKERS - (GROUP - 1) * g, SHARE)
-
-    def far_first(j):
-        return lax.rem(me + CELLS // 2 + (j + 1) // 2 * (1 - 2 * lax.rem(j, 2)), CELLS)
-
-    barrier = pltpu.get_barrier_semaphore()
-
-    def greet(j, carry):
-        pl.semaphore_signal(
-            barrier, inc=1, device_id={"cell": far_first(j)}, device_id_type=MESH
-        )
-        return carry
-
-    def greet_aux(j, carry):
-        pl.semaphore_signal(
-            barrier, inc=1, device_id={"aux": lax.rem(my_aux + 2 * j, AUX)}, device_id_type=MESH
-        )
-        return carry
-
-    lax.fori_loop(0, CELLS - 1, greet, 0)
-    lax.fori_loop(1, AUX // 2, greet_aux, 0)
-    pl.semaphore_signal(barrier, inc=1, device_id={"aux": partner}, device_id_type=MESH)
 
     occ_loads = [pltpu.make_async_copy(occ.at[:, t, :], occ_v.at[t], load_sem.at[t]) for t in range(2)]
     block_loads = [pltpu.make_async_copy(blocks.at[:, p, :], blocks_v.at[p], load_sem.at[2 + p]) for p in range(ROWS)]
@@ -140,8 +137,29 @@
     vir_load.start()
     for load in occ_loads + block_loads:
         load.start()
+
+
+    barrier = pltpu.get_barrier_semaphore()
+
+    def greet(j, carry):
+        for offset in (SIDE - j, SIDE + j):
+            pl.semaphore_signal(
+                barrier, inc=1, device_id={"cell": wrapped(me + offset, CELLS)}, device_id_type=MESH
+            )
+        return carry
+
+    def greet_aux(j, carry):
+        pl.semaphore_signal(
+            barrier, inc=1, device_id={"aux": lax.rem(my_aux + 2 * j, AUX)}, device_id_type=MESH
+        )
+        return carry
+
+    pl.semaphore_signal(barrier, inc=1, device_id={"cell": wrapped(me + SIDE, CELLS)}, device_id_type=MESH)
+    lax.fori_loop(1, SIDE, greet, 0)
+    lax.fori_loop(1, AUX // 2, greet_aux, 0)
+    pl.semaphore_signal(barrier, inc=1, device_id={"aux": partner}, device_id_type=MESH)
+
     cells_load.wait()
-
     folded = cells_v[...] & 3
     number = folded[0:1] * 16 + folded[1:2] * 4 + folded[2:3]
     wanted = lax.broadcasted_iota(jnp.int32, (CELLS, CELLS), 0)
@@ -218,23 +236,30 @@
         return sent_half[part].at[pl.ds(pl.multiple_of(slot * 8, 8), 8)]
 
     def send_half(part):
-        def one(j, carry):
-            peer = far_first(j)
-
-            @pl.when(lax.rem(peer, GROUP) != GROUP - 1)
-            def _():
-                pltpu.make_async_remote_copy(
-                    src_ref=half_source(part, peer - peer // GROUP),
-                    dst_ref=got_half[part].at[me],
-                    send_sem=half_send.at[part],
-                    recv_sem=half_recv.at[part],
-                    device_id={"cell": peer},
-                    device_id_type=MESH,
-                ).start()
-
-            return carry
-
-        lax.fori_loop(0, CELLS - 1, one, 0)
+        for turn in (2, 3, 1, 0):
+            block = wrapped(my_block + turn, 4)
+
+            def one(j, carry):
+                m = wrapped(j + my_first, GROUP - 1)
+                peer = block * GROUP + m
+
+                def send():
+                    pltpu.make_async_remote_copy(
+                        src_ref=half_source(part, block * (GROUP - 1) + m),
+                        dst_ref=got_half[part].at[me],
+                        send_sem=half_send.at[part],
+                        recv_sem=half_recv.at[part],
+                        device_id={"cell": peer},
+                        device_id_type=MESH,
+                    ).start()
+
+                if turn:
+                    send()
+                else:
+                    pl.when(peer != me)(send)
+                return carry
+
+            lax.fori_loop(0, GROUP - 1, one, 0)
 
         @pl.when(active)
         def _():
@@ -264,19 +289,17 @@
     def send_spec(part, g):
         sources, target, sem = spec_copy(part, g)
 
-        def one(j, carry):
-            peer, _ = member(g, j)
+        def send(peer, u):
             pltpu.make_async_remote_copy(
-                src_ref=sources.at[lax.rem(peer, SIDE)],
+                src_ref=sources.at[wrapped(peer, SIDE)],
                 dst_ref=target,
                 send_sem=spec_send.at[sem],
                 recv_sem=spec_recv.at[sem],
                 device_id={"cell": peer},
                 device_id_type=MESH,
             ).start()
-            return carry
-
-        lax.fori_loop(0, SIDE - 1, one, 0)
+
+        for_members(g, send)
         pltpu.make_async_copy(sources.at[my_low], target, spec_local.at[sem]).start()
 
     def fourier(part):
@@ -424,8 +447,7 @@
                             chunk = jnp.where(lane < shift, chunk, pltpu.roll(wide(base + m), shift, 1))
                     sent_pairs[g, block * GROUP + m, side] = chunk
 
-        def one(j, carry):
-            peer, u = member(g, j)
+        def send(peer, u):
             pltpu.make_async_remote_copy(
                 src_ref=sent_pairs.at[g, u],
                 dst_ref=out[g].at[my_low],
@@ -434,11 +456,9 @@
                 device_id={"cell": peer},
                 device_id_type=MESH,
             ).start()
-            return carry
-
-        lax.fori_loop(0, SIDE - 1, one, 0)
-        my_place = lax.rem(me + CELLS - GROUP * g, SIDE)
-        pltpu.make_async_copy(sent_pairs.at[g, my_place], out[g].at[my_low], pair_local.at[g]).start()
+
+        for_members(g, send)
+        pltpu.make_async_copy(sent_pairs.at[g, share_at[g]], out[g].at[my_low], pair_local.at[g]).start()
 
     for g in range(2):
         band_and_pairs(g)

time: 60.2 us -> 58.8 us (0.977)
  Pallas kernels: 60 us -> 58.6 us
    pallas_call x1, Pallas kernels: 58.3 us -> 56.9 us  [exchange(): pl.pallas_call(kernel, out_shape=(pairs, pairs), in_specs=[pl.BlockSpec(m...]
where the time goes in v4:
time: 58.8 us; the launch traced here: 58.6 us
  Pallas kernels  58.6 us (100%)
    pallas_call x1, Pallas kernels, exchange(): pl.pallas_call(kernel, out_shape=(pairs, pairs), in_specs=[pl.BlockSpec(m...  56.9 us
    pallas_call x1, Pallas kernels, reorder(): pl.pallas_call(reorder_kernel, out_shape=jax.ShapeDtypeStruct((2, ROWS, C...  1.72 us

profile of v4, /device:TPU:1, one launch (start us, length us, event | category | flops | bytes accessed | tf_op | source)
XLA Modules:
  0.0 58.6 jit_solution(13543714851428676976)
XLA Ops:
  0.0 0.0 copy-start
  0.0 56.9 %transform.1 = (f32[32,2,4,256]{3,2,1,0:T(4,128)S(1)}, f32[32,2,4,256]{3,2,1,0:T(4,128)S(1)}) custom-call(s32[3,64]{1,0:T(4,128)} %cells.1, f32[300,4,300]{2,1,0:T(4,128)} %bitcast.7, f32[60,2,300]{2,1,0:T(2,128)} %bitcast.8, f32[30,2,300]{2,1,0:T(2,128)} %bitcast.9), custom_call_target="tpu_custom_call" | custom-call | tf_op jit(solution)/shard_map/transform/pallas_call | solution.py:497
  56.9 0.0 copy-done
  56.9 1.7 %reorder.1 = f32[2,4,64,225]{3,2,1,0:T(8,128)} custom-call(s32[64]{0:T(128)S(1)} %copy-done, f32[32,2,4,256]{3,2,1,0:T(4,128)S(1)} %get-tuple-element.7.got_0, f32[32,2,4,256]{3,2,1,0:T(4,128)S(1)} %get-tuple-element.8.got_1), custom_call_target="tpu_custom_call" | custom-call | tf_op jit(solution)/shard_map/reorder/pallas_call | solution.py:588
Async XLA Ops:
  0.0 56.9 %copy-start = (s32[64]{0:T(128)S(1)}, s32[64]{0:T(128)}, u32[]{:S(2)}) copy-start(s32[64]{0:T(128)} %transfer.1) | copy-start | bytes 772

commit v5 on v4

--- a/solution.py
+++ b/solution.py
@@ -155,7 +155,8 @@
         return carry
 
     pl.semaphore_signal(barrier, inc=1, device_id={"cell": wrapped(me + SIDE, CELLS)}, device_id_type=MESH)
-    lax.fori_loop(1, SIDE, greet, 0)
+    for j in range(1, SIDE):
+        greet(j, 0)
     lax.fori_loop(1, AUX // 2, greet_aux, 0)
     pl.semaphore_signal(barrier, inc=1, device_id={"aux": partner}, device_id_type=MESH)
 

time: 58.8 us -> 59.3 us (level)
  no operation moved by 1% of the time
where the time goes in v5:
time: 59.3 us; the launch traced here: 59.1 us
  Pallas kernels  59.1 us (100%)
    pallas_call x1, Pallas kernels, exchange(): pl.pallas_call(kernel, out_shape=(pairs, pairs), in_specs=[pl.BlockSpec(m...  57.4 us
    pallas_call x1, Pallas kernels, reorder(): pl.pallas_call(reorder_kernel, out_shape=jax.ShapeDtypeStruct((2, ROWS, C...  1.72 us

profile of v5, /device:TPU:1, one launch (start us, length us, event | category | flops | bytes accessed | tf_op | source)
XLA Modules:
  0.0 59.1 jit_solution(8962803519547105835)
XLA Ops:
  0.0 0.0 copy-start
  0.0 57.4 %transform.1 = (f32[32,2,4,256]{3,2,1,0:T(4,128)S(1)}, f32[32,2,4,256]{3,2,1,0:T(4,128)S(1)}) custom-call(s32[3,64]{1,0:T(4,128)} %cells.1, f32[300,4,300]{2,1,0:T(4,128)} %bitcast.7, f32[60,2,300]{2,1,0:T(2,128)} %bitcast.8, f32[30,2,300]{2,1,0:T(2,128)} %bitcast.9), custom_call_target="tpu_custom_call" | custom-call | tf_op jit(solution)/shard_map/transform/pallas_call | solution.py:498
  57.4 0.0 copy-done
  57.4 1.7 %reorder.1 = f32[2,4,64,225]{3,2,1,0:T(8,128)} custom-call(s32[64]{0:T(128)S(1)} %copy-done, f32[32,2,4,256]{3,2,1,0:T(4,128)S(1)} %get-tuple-element.7.got_0, f32[32,2,4,256]{3,2,1,0:T(4,128)S(1)} %get-tuple-element.8.got_1), custom_call_target="tpu_custom_call" | custom-call | tf_op jit(solution)/shard_map/reorder/pallas_call | solution.py:589
Async XLA Ops:
  0.0 57.4 %copy-start = (s32[64]{0:T(128)S(1)}, s32[64]{0:T(128)}, u32[]{:S(2)}) copy-start(s32[64]{0:T(128)} %transfer.1) | copy-start | bytes 772
